TPU v7x, 32 devices: a whole 2x2x4 slice. The times are simulated.
32 devices in a mesh: blk: 8 (over y, x, core), seq: 4 (over z).
Axes of the slice: x: 2, y: 2, z: 4, core: 2. Of those that a mesh axis runs over, the one named last changes fastest.
Arguments:
- layer_input: bfloat16 [8, 512, 8192], P('blk', 'seq'), may hold values from -6 to 6
- queries: bfloat16 [8, 512, 4096], P('blk', 'seq'), may hold values from -48 to 48, as said below
- grad_out: bfloat16 [8, 512, 4096], P('blk', 'seq'), may hold values from -6 to 6
- segment_ids: int32 [8, 512], P('blk', 'seq'), may hold values from 0 to 3, never falling along the last dimension, each value on 1 to 256 neighbouring positions
- kv_weight: bfloat16 [8192, 1024], P(('blk', 'seq')), may hold values from -0.0625 to 0.0625
- norm_gain: float32 [8192], replicated, may hold values from 0.5 to 1.5
Outputs:
- attended: bfloat16 [8, 512, 4096], P('blk', 'seq')
- grad_queries: bfloat16 [8, 512, 4096], P('blk', 'seq')
- grad_input: bfloat16 [8, 512, 8192], P('blk', 'seq')
- grad_weight: float32 [8192, 1024], P(('blk', 'seq'))
- grad_gain: float32 [8192], replicated
Inputs may be any that keep to these rules, and one draw needn't show every extreme that they name: Projected queries; some rows may be larger than others.
All inputs are finite; a program needn't handle non-finite values.
Results may differ from a plain program's by a relative error of at most 0.02.
The roundings to bfloat16 on the way count: a program that leaves them out, or rounds other values in their place, can miss the bound.
Values may be sent and summed in bfloat16 or wider, within the bound.
A program may use at most 128 MiB of HBM per device.

v0:
```python
import math

import jax
import jax.numpy as jnp
from jax import lax
from jax.sharding import PartitionSpec as P

HEAD = 128


epsilon = 1e-05


def fold_local(step_fn, initial, kv_rows, doc_rows):
    key_block = math.gcd(kv_rows.shape[0], 512)
    steps_count = kv_rows.shape[0] // key_block

    def fold_turn(state_now, position):
        offset = position * key_block
        shard_piece = (
            lax.dynamic_slice_in_dim(kv_rows, offset, key_block, 0),
            lax.dynamic_slice_in_dim(doc_rows, offset, key_block, 0),
        )
        return (step_fn(state_now, shard_piece, offset), None)

    return lax.scan(fold_turn, initial, jnp.arange(steps_count, dtype=jnp.int32))[0]


def shards(layer_input, queries, grad_out, segment_ids, kv_weight, norm_gain):
    f32 = jnp.float32
    tok_rows = layer_input.shape[1]
    model_width = layer_input.shape[2]
    seq_devices = lax.axis_size("seq")
    blk_devices = lax.axis_size("blk")
    length = tok_rows * seq_devices
    seq_index = lax.axis_index("seq")
    kv_total = kv_weight.shape[1]
    kv_width = kv_total // 2
    kv_heads = kv_width // HEAD
    query_count = queries.shape[2] // HEAD
    group_size = query_count // kv_heads
    score_scale = HEAD ** (-0.5)
    piece_cols = kv_weight.shape[0]
    source = layer_input[0].astype(f32)
    inv_rms = lax.rsqrt(jnp.mean(source * source, axis=1, keepdims=True) + epsilon)
    scaled = source * inv_rms
    normed = (scaled * norm_gain).astype(jnp.bfloat16)
    split_cols = normed.reshape(tok_rows, blk_devices, seq_devices, piece_cols)
    columns = lax.all_to_all(split_cols, "seq", split_axis=2, concat_axis=0, tiled=True).reshape(
        length, blk_devices * piece_cols
    )
    weight_slab = lax.all_gather(kv_weight, "blk", axis=0, tiled=True)
    query_heads = queries[0].reshape(tok_rows, kv_heads, group_size, HEAD)
    query_pos = seq_index * tok_rows + jnp.arange(tok_rows, dtype=jnp.int32)
    query_doc = segment_ids[0]
    grad_heads = grad_out[0].reshape(tok_rows, kv_heads, group_size, HEAD).transpose(1, 2, 0, 3)

    def scores_of(kv_piece, doc_piece, offset):
        rows_here = kv_piece.shape[0]
        key_heads = kv_piece[:, :kv_width].reshape(rows_here, kv_heads, HEAD)
        raw_scores = (
            jnp.einsum("qgjd,kgd->gjqk", query_heads, key_heads, preferred_element_type=f32)
            * score_scale
        )
        key_pos = offset + jnp.arange(rows_here, dtype=jnp.int32)
        allowed = (key_pos[None, :] <= query_pos[:, None]) & (
            doc_piece[None, :] == query_doc[:, None]
        )
        return (jnp.where(allowed, raw_scores, -1e30), allowed, key_heads)

    def forward_step(state_now, shard_piece, offset):
        row_max, row_sum, weighted = state_now
        kv_piece, doc_piece = shard_piece
        rows_here = kv_piece.shape[0]
        masked, allowed, key_heads = scores_of(kv_piece, doc_piece, offset)
        new_max = jnp.maximum(row_max, jnp.max(masked, axis=-1, keepdims=True))
        factor = jnp.exp(row_max - new_max)
        expo_terms = jnp.where(allowed, jnp.exp(masked - new_max), 0.0)
        value_heads = kv_piece[:, kv_width:].reshape(rows_here, kv_heads, HEAD)
        weights = expo_terms.astype(jnp.bfloat16)
        weighted = weighted * factor + jnp.einsum(
            "gjqk,kgd->gjqd", weights, value_heads, preferred_element_type=f32
        )
        row_sum = row_sum * factor + jnp.sum(expo_terms, axis=-1, keepdims=True)
        return (new_max, row_sum, weighted)

    stat_shape = (kv_heads, group_size, tok_rows, 1)
    initial = (
        jnp.full(stat_shape, -1e30, f32),
        jnp.zeros(stat_shape, f32),
        jnp.zeros((kv_heads, group_size, tok_rows, HEAD), f32),
    )
    full_terms = jnp.dot(columns, weight_slab, preferred_element_type=f32)
    kv_all = lax.psum(full_terms, "seq").astype(jnp.bfloat16)
    doc_all = lax.all_gather(query_doc, "seq", axis=0, tiled=True)
    row_max, row_sum, weighted = fold_local(forward_step, initial, kv_all, doc_all)
    summed = weighted / row_sum
    attended = (
        summed.transpose(2, 0, 1, 3).reshape(tok_rows, query_count * HEAD).astype(jnp.bfloat16)
    )
    log_total = row_max + jnp.log(row_sum)
    attended_heads = attended.reshape(tok_rows, kv_heads, group_size, HEAD).transpose(1, 2, 0, 3)
    row_delta = jnp.sum(grad_heads.astype(f32) * attended_heads.astype(f32), axis=-1, keepdims=True)

    def backward_step(state_now, shard_piece, offset):
        grad_query, grad_rows = state_now
        kv_piece, doc_piece = shard_piece
        rows_here = kv_piece.shape[0]
        masked, allowed, key_heads = scores_of(kv_piece, doc_piece, offset)
        softmax_probs = jnp.where(allowed, jnp.exp(masked - log_total), 0.0)
        value_heads = kv_piece[:, kv_width:].reshape(rows_here, kv_heads, HEAD)
        grad_probs = jnp.einsum(
            "gjqd,kgd->gjqk", grad_heads, value_heads, preferred_element_type=f32
        )
        grad_scores = (softmax_probs * (grad_probs - row_delta)).astype(jnp.bfloat16)
        probs_half = softmax_probs.astype(jnp.bfloat16)
        grad_values = jnp.einsum(
            "gjqk,gjqd->kgd", probs_half, grad_heads, preferred_element_type=f32
        )
        grad_keys = (
            jnp.einsum("gjqk,qgjd->kgd", grad_scores, query_heads, preferred_element_type=f32)
            * score_scale
        )
        grad_query = (
            grad_query
            + jnp.einsum("gjqk,kgd->qgjd", grad_scores, key_heads, preferred_element_type=f32)
            * score_scale
        )
        new_rows = jnp.concatenate(
            [grad_keys.reshape(rows_here, kv_width), grad_values.reshape(rows_here, kv_width)],
            axis=1,
        )
        current = lax.dynamic_slice_in_dim(grad_rows, offset, rows_here, 0)
        grad_rows = lax.dynamic_update_slice_in_dim(grad_rows, current + new_rows, offset, 0)
        return (grad_query, grad_rows)

    back_initial = (
        jnp.zeros((tok_rows, kv_heads, group_size, HEAD), f32),
        jnp.zeros((length, kv_total), f32),
    )
    grad_query, grad_rows = fold_local(backward_step, back_initial, kv_all, doc_all)
    grad_kv = lax.psum(grad_rows, "seq").astype(jnp.bfloat16)
    grad_queries = grad_query.reshape(tok_rows, query_count * HEAD).astype(jnp.bfloat16)
    slab_back = lax.all_gather(kv_weight, "blk", axis=0, tiled=True)
    grad_weight = lax.psum_scatter(
        lax.dot_general(columns, grad_kv, (((0,), (0,)), ((), ())), preferred_element_type=f32),
        "blk",
        scatter_dimension=0,
        tiled=True,
    )
    grad_cols = lax.dot_general(
        grad_kv, slab_back, (((1,), (1,)), ((), ())), preferred_element_type=f32
    ).astype(jnp.bfloat16)
    grad_cols = grad_cols.reshape(length, blk_devices, 1, piece_cols)
    grad_normed = lax.all_to_all(grad_cols, "seq", split_axis=0, concat_axis=2, tiled=True).reshape(
        tok_rows, model_width
    )
    grad_norm = grad_normed.astype(f32)
    grad_gain = lax.psum(jnp.sum(grad_norm * scaled, axis=0), ("blk", "seq"))
    grad_hat = grad_norm * norm_gain
    grad_input = inv_rms * (grad_hat - scaled * jnp.mean(grad_hat * scaled, axis=1, keepdims=True))
    return (
        attended[None],
        grad_queries[None],
        grad_input.astype(jnp.bfloat16)[None],
        grad_weight,
        grad_gain,
    )


def solution(mesh):
    in_specs = (
        P("blk", "seq", None),
        P("blk", "seq", None),
        P("blk", "seq", None),
        P("blk", "seq"),
        P(("blk", "seq"), None),
        P(),
    )
    out_specs = (
        P("blk", "seq", None),
        P("blk", "seq", None),
        P("blk", "seq", None),
        P(("blk", "seq"), None),
        P(),
    )
    return jax.shard_map(shards, mesh=mesh, in_specs=in_specs, out_specs=out_specs, check_vma=False)
```

profile of v0, /device:TPU:0, one launch (start us, length us, event | category | flops | bytes accessed | tf_op | source)
XLA Modules:
  0.0 391.9 jit_solution(7872189699810399618)
XLA Ops:
  8.7 6.0 %reshape.228 = f32[128,8,4,256]{3,2,1,0:T(4,128)} reshape(bf16[1,128,8192]{2,1,0:T(8,128)(2,1)} %param.6) | data formatting | bytes 6291456 | tf_op jit(solution)/shard_map/convert_element_type | solution.py:44
  15.2 4.3 %fusion.6 = bf16[128,8,4,256]{3,1,0,2:T(8,128)(2,1)} fusion(f32[128,8,4,256]{3,2,1,0:T(4,128)} %reshape.228, f32[8,4,256]{2,0,1:T(8,128)S(1)} %copy.101, f32[128]{0:T(128)S(1)} %add_rsqrt_fusion), kind=kLoop, calls=%fused_computation.13 | loop fusion | flops 3145728 | bytes 6324736 | tf_op jit(solution)/shard_map/convert_element_type | solution.py:47
  19.5 6.5 %all-to-all-start = ((bf16[128,8,4,256]{3,1,0,2:T(8,128)(2,1)}), bf16[128,8,4,256]{3,1,0,2:T(8,128)(2,1)}, u32[]{:S(2)}, u32[]{:S(2)}) async-start(bf16[128,8,4,256]{3,1,0,2:T(8,128)(2,1)} %fusion.6), calls=%async_computation | async-start | bytes 4194304 | tf_op jit(solution)/shard_map/all_to_all | solution.py:49
  27.6 2.3 copy.106
  29.9 35.9 %all-gather = s32[1,512]{1,0:T(1,128)S(1)} all-gather(s32[1,128]{1,0:T(1,128)S(1)} %copy-done.8), channel_id=2, replica_groups=mesh['blk'=8,'seq'=4] {'seq'}, dimensions={1}, use_global_device_ids=true | all-gather | bytes 2560 | tf_op jit(solution)/shard_map/all_gather | solution.py:95
  65.9 8.4 %all-to-all-done = bf16[128,8,4,256]{3,1,0,2:T(8,128)(2,1)} async-done(((bf16[128,8,4,256]{3,1,0,2:T(8,128)(2,1)}), bf16[128,8,4,256]{3,1,0,2:T(8,128)(2,1)}, u32[]{:S(2)}, u32[]{:S(2)}) %all-to-all-start) | async-done | bytes 2097184 | tf_op jit(solution)/shard_map/all_to_all | solution.py:49
  74.3 3.6 copy.141
  77.9 6.5 %fusion.31 = f32[512,1024]{1,0:T(8,128)} fusion(bf16[512,2048]{1,0:T(8,128)(2,1)} %bitcast.108, bf16[2048,1024]{1,0:T(8,128)(2,1)} %all-gather.3.cloned.1.call-done), kind=kOutput, calls=%fused_computation.56 | convolution fusion | flops 2147483648 | bytes 8388608 | tf_op jit(solution)/shard_map/dot_general | solution.py:93
  84.4 75.7 %all-reduce.2 = bf16[512,1024]{1,0:T(8,128)(2,1)} all-reduce(f32[512,1024]{1,0:T(8,128)} %fusion.31), channel_id=1, replica_groups=mesh['blk'=8,'seq'=4] {'seq'}, use_global_device_ids=true, to_apply=%region_1.0 | all-reduce | flops 524288 | bytes 3145728 | tf_op jit(solution)/shard_map/psum | solution.py:94
  160.1 2.2 fusion.30
  164.3 2.1 copy.126
  166.4 2.5 fusion.4
  168.9 2.2 fusion.1
  172.1 2.0 reshape.224
  174.1 5.9 %fusion.9 = f32[4,512,128,1]{1,2,3,0:T(8,128)S(1)} fusion(bf16[4,8,128,128]{2,3,1,0:T(8,128)(2,1)} %bitcast.105, f32[4,512,128,8]{2,1,3,0:T(8,128)} %copy-done, f32[4,8,128]{2,1,0:T(8,128)S(1)} %get-tuple-element.99, pred[128,512]{0,1:T(8,128)(4,1)S(1)} %fusion.21), kind=kOutput, calls=%fused_computation.19 | convolution fusion | flops 547356672 | bytes 10567680 | tf_op jit(solution)/shard_map/while/body/eval_jaxpr/gjqk,gjqd->kgd/dot_general | solution.py:117
  180.2 3.2 fusion.14
  184.0 3.1 fusion
  190.6 71.4 %all-reduce.3 = bf16[512,1024]{0,1:T(8,128)(2,1)S(1)} all-reduce(f32[512,1024]{0,1:T(8,128)} %pad_maximum_fusion), channel_id=1, replica_groups=mesh['blk'=8,'seq'=4] {'seq'}, use_global_device_ids=true, to_apply=%region_5.6 | all-reduce | flops 524288 | bytes 3145728 | tf_op jit(solution)/shard_map/psum | solution.py:142
  262.0 7.2 %fusion.32 = f32[2048,1024]{1,0:T(8,128)} fusion(bf16[512,2048]{1,0:T(8,128)(2,1)} %bitcast.109, bf16[512,1024]{0,1:T(8,128)(2,1)S(1)} %all-reduce.3), kind=kOutput, calls=%fused_computation.57 | convolution fusion | flops 2147483648 | bytes 11534336 | tf_op jit(solution)/shard_map/dot_general | solution.py:146
  269.2 4.6 %convolution_convert_fusion = bf16[512,2048]{1,0:T(8,128)(2,1)S(1)} fusion(bf16[2048,1024]{1,0:T(8,128)(2,1)} %all-gather.3.cloned.1.call-done, bf16[512,1024]{0,1:T(8,128)(2,1)S(1)} %all-reduce.3), kind=kOutput, calls=%fused_computation.22 | convolution fusion | flops 2148532224 | bytes 7340032 | tf_op jit(solution)/shard_map/dot_general | solution.py:151
  273.8 2.0 copy.142
  275.8 4.9 %all-to-all-start.1 = ((bf16[512,8,1,256]{3,1,2,0:T(8,128)(2,1)}), bf16[512,8,1,256]{3,1,2,0:T(8,128)(2,1)}, u32[]{:S(2)}, u32[]{:S(2)}) async-start(bf16[512,8,1,256]{3,1,2,0:T(8,128)(2,1)} %bitcast.102), calls=%async_computation.1 | async-start | bytes 4194304 | tf_op jit(solution)/shard_map/all_to_all | solution.py:155
  280.7 4.6 %reshape.230 = f32[128,8,4,1,256]{4,2,1,0,3:T(4,128)} reshape(bf16[1,128,8192]{2,1,0:T(8,128)(2,1)S(1)} %copy-done.3) | data formatting | bytes 6291456 | tf_op jit(solution)/shard_map/convert_element_type | solution.py:44
  285.3 4.2 %multiply_convert_fusion.1 = bf16[4,128,8,128]{3,1,2,0:T(8,128)(2,1)} fusion(bf16[512,4,128,1]{0,2,3,1:T(8,128)(2,1)S(1)} %copy-done.4, bf16[4,8,128,512]{2,3,1,0:T(8,128)(2,1)} %copy-done.2), kind=kOutput, calls=%fused_computation.27 | convolution fusion | flops 537919488 | bytes 5767168 | tf_op jit(solution)/shard_map/while/body/eval_jaxpr/gjqk,kgd->qgjd/dot_general | solution.py:126
  289.6 2.3 copy.120
  291.8 2.3 copy.119
  294.1 30.7 %all-to-all-done.1 = bf16[512,8,1,256]{3,1,2,0:T(8,128)(2,1)} async-done(((bf16[512,8,1,256]{3,1,2,0:T(8,128)(2,1)}), bf16[512,8,1,256]{3,1,2,0:T(8,128)(2,1)}, u32[]{:S(2)}, u32[]{:S(2)}) %all-to-all-start.1) | async-done | bytes 2097184 | tf_op jit(solution)/shard_map/all_to_all | solution.py:155
  326.7 4.6 %copy.115 = f32[128,8,4,1,256]{4,2,1,0,3:T(4,128)} copy(f32[128,8,4,1,256]{4,1,0,2,3:T(8,128)S(1)} %convert_bitcast_fusion) | data formatting | bytes 8388608 | tf_op jit(solution)/shard_map/convert_element_type | solution.py:158
  331.3 5.8 %reshape.229 = f32[1,128,8192]{2,1,0:T(8,128)} reshape(f32[128,8,4,1,256]{4,2,1,0,3:T(4,128)} %copy.115) | data formatting | bytes 8388608 | tf_op jit(solution)/shard_map/convert_element_type | solution.py:158
  337.2 4.9 %multiply_reduce_fusion = (f32[8,4,256]{2,0,1:T(8,128)S(1)}, f32[128]{0:T(128)S(1)}) fusion(f32[128,8,4,1,256]{4,2,1,0,3:T(4,128)} %reshape.230, bf16[4,128,8,1,256]{4,2,1,0,3:T(8,128)(2,1)} %bitcast.30, f32[128]{0:T(128)S(1)} %add_rsqrt_fusion, f32[8,4,256]{2,0,1:T(8,128)S(1)} %copy.101), kind=kLoop, calls=%fused_computation.14 | loop fusion | flops 7331712 | bytes 6358016 | tf_op jit(solution)/shard_map/reduce_sum | solution.py:159
  342.1 38.5 %psum.23 = f32[8192]{0:T(1024)} all-reduce(f32[8192]{0:T(1024)S(1)} %bitcast.117), channel_id=1, replica_groups=mesh['blk'=8,'seq'=4] {'blk','seq'}, use_global_device_ids=true, to_apply=%region_9.10 | all-reduce | flops 8192 | bytes 65536 | tf_op jit(solution)/shard_map/psum | solution.py:159
  380.6 4.5 %multiply_convert_fusion = bf16[1,128,8192]{2,1,0:T(8,128)(2,1)} fusion(f32[1,128,8192]{2,1,0:T(8,128)} %reshape.229, bf16[1,128,8192]{2,1,0:T(8,128)(2,1)S(1)} %copy-done.3, f32[128]{0:T(128)S(1)} %broadcast_multiply_fusion, f32[8192]{0:T(1024)S(1)} %copy-done.7, f32[128]{0:T(128)S(1)} %add_rsqrt_fusion), kind=kLoop, calls=%fused_computation.15 | loop fusion | flops 7340032 | bytes 8422400 | tf_op jit(solution)/shard_map/convert_element_type | solution.py:165
  (42 shorter events, 13.1 us)
Async XLA Ops:
  7.2 7.6 %copy-start.3 = (bf16[1,128,8192]{2,1,0:T(8,128)(2,1)S(1)}, bf16[1,128,8192]{2,1,0:T(8,128)(2,1)}, u32[]{:S(2)}) copy-start(bf16[1,128,8192]{2,1,0:T(8,128)(2,1)} %param.6) | copy-start | bytes 6291460
  7.2 70.7 %all-gather.3.cloned.1.call-start = ((), (), s32[]{:S(2)}) async-start(), calls=%async_computation.3 | async-start | bytes 4718592 | tf_op jit(solution)/shard_map/all_gather | solution.py:52
  19.5 10.4 %copy-start.8 = (s32[1,128]{1,0:T(1,128)S(1)}, s32[1,128]{1,0:T(1,128)}, u32[]{:S(2)}) copy-start(s32[1,128]{1,0:T(1,128)} %param.9) | copy-start | bytes 1540
  19.5 54.8 %all-to-all-start = ((bf16[128,8,4,256]{3,1,0,2:T(8,128)(2,1)}), bf16[128,8,4,256]{3,1,0,2:T(8,128)(2,1)}, u32[]{:S(2)}, u32[]{:S(2)}) async-start(bf16[128,8,4,256]{3,1,0,2:T(8,128)(2,1)} %fusion.6), calls=%async_computation | async-start | bytes 4194304 | tf_op jit(solution)/shard_map/all_to_all | solution.py:49
  26.0 359.1 %reduce-scatter.2.cloned.1.call-start = ((), (), s32[]{:S(2)}) async-start(), calls=%async_computation.4 | async-start | bytes 9437184 | tf_op jit(solution)/shard_map/reduce_scatter | solution.py:145
  168.9 3.2 copy-start
  174.1 6.1 %copy-start.1 = (f32[4,512,128,8]{2,1,3,0:T(8,128)S(1)}, f32[4,512,128,8]{2,1,3,0:T(8,128)}, u32[]{:S(2)}) copy-start(f32[4,512,128,8]{2,1,3,0:T(8,128)} %copy-done) | copy-start | bytes 25165828
  174.1 6.1 %copy-start.6 = (bf16[512,4,128]{2,1,0:T(4,128)(2,1)S(1)}, bf16[512,4,128]{2,1,0:T(4,128)(2,1)}, u32[]{:S(2)}) copy-start(bf16[512,4,128]{2,1,0:T(4,128)(2,1)} %reshape.224) | copy-start | bytes 1572868
  180.2 3.2 copy-start.5
  187.1 2.0 copy-start.2
  275.8 48.9 %all-to-all-start.1 = ((bf16[512,8,1,256]{3,1,2,0:T(8,128)(2,1)}), bf16[512,8,1,256]{3,1,2,0:T(8,128)(2,1)}, u32[]{:S(2)}, u32[]{:S(2)}) async-start(bf16[512,8,1,256]{3,1,2,0:T(8,128)(2,1)} %bitcast.102), calls=%async_computation.1 | async-start | bytes 4194304 | tf_op jit(solution)/shard_map/all_to_all | solution.py:155
  280.7 4.6 %copy-start.4 = (bf16[512,4,128,1]{0,2,3,1:T(8,128)(2,1)S(1)}, bf16[512,4,128,1]{0,2,3,1:T(8,128)(2,1)}, u32[]{:S(2)}) copy-start(bf16[512,4,128,1]{0,2,3,1:T(8,128)(2,1)} %copy.126) | copy-start | bytes 1572868
  337.2 43.5 %copy-start.7 = (f32[8192]{0:T(1024)S(1)}, f32[8192]{0:T(1024)}, u32[]{:S(2)}) copy-start(f32[8192]{0:T(1024)} %param.11) | copy-start | bytes 98308
Sparse Core Ops, SparseCore 0:
  9.9 39.2 all-gather.2
  269.3 72.8 reduce-scatter.1
where the time goes:
time: 394 us; the launch traced here: 392 us
  blocking collectives  221 us (56%)
  local copies, waits for them, and re-layouts  45.9 us (12%)
  waiting for transfers between devices  39.7 us (10%)
  matrix products  38.6 us (10%)
  other arithmetic  20.6 us (5%)
  between operations  14.2 us (4%)
  starting transfers between devices  11.5 us (3%)
    psum x1, blocking collectives, shards(): kv_all = lax.psum(full_terms, 'seq').astype(jnp.bfloat16)  75.7 us
    psum x1, blocking collectives, shards(): grad_kv = lax.psum(grad_rows, 'seq').astype(jnp.bfloat16)  71.4 us
    psum x1, blocking collectives, shards(): grad_gain = lax.psum(jnp.sum(grad_norm * scaled, axis=0), ('blk', 'seq'))  38.5 us
    all_gather x1, blocking collectives, shards(): doc_all = lax.all_gather(query_doc, 'seq', axis=0, tiled=True)  35.9 us
    all_to_all x1, waiting for transfers between devices, shards(): lax.all_to_all(grad_cols, 'seq', split_axis=0, concat_axis=2, tiled=True)  30.7 us
    unnamed x24, local copies, waits for them, and re-layouts  14.1 us
    convert_element_type x2, local copies, waits for them, and re-layouts, shards(): source = layer_input[0].astype(f32)  10.6 us
    convert_element_type x2, local copies, waits for them, and re-layouts, shards(): grad_norm = grad_normed.astype(f32)  10.5 us
  transfers between devices with their start and end apart: 4, of which 2 were waited for; matrix products, arithmetic and copies ran while one was open for 16% of the time, Pallas kernels for 0%

commit v1 on v0

v1 whole, which is shorter than its diff:
```python
import functools

import jax
import jax.numpy as jnp
from jax import lax
from jax.experimental import pallas as pl
from jax.experimental.pallas import tpu as pltpu
from jax.sharding import PartitionSpec as P

HEAD = 128
EPSILON = 1e-05
F32 = jnp.float32
BF16 = jnp.bfloat16
MESH = pl.DeviceIdType.MESH
VMEM_LIMIT = 60 * 1024 * 1024


def remote(src, dst, send_sem, recv_sem, **where):
    return pltpu.make_async_remote_copy(
        src_ref=src,
        dst_ref=dst,
        send_sem=send_sem,
        recv_sem=recv_sem,
        device_id=where,
        device_id_type=MESH,
    )


def greet(n, m):
    s = lax.axis_index("seq")
    b = lax.axis_index("blk")
    barrier = pltpu.get_barrier_semaphore()
    for j in range(1, n):
        pl.semaphore_signal(
            barrier, inc=1, device_id={"seq": lax.rem(s + j, n)}, device_id_type=MESH
        )
    for j in range(1, m):
        pl.semaphore_signal(
            barrier, inc=1, device_id={"blk": lax.rem(b + j, m)}, device_id_type=MESH
        )
    pl.semaphore_wait(barrier, n - 1 + m - 1)


class Layout:
    def __init__(self, n, m, piece):
        self.n, self.m, self.piece = n, m, piece
        self.wide = m * piece
        self.direct = piece % 128 == 0
        self.unit = piece if self.direct else 256
        self.units = self.wide // self.unit

    def row(self, sp, t):
        return t * self.n + sp if self.direct else sp * self.units + t

    def cols(self, sp, t):
        return pl.ds(pl.multiple_of(self.row(sp, t) * self.unit, 128), self.unit)

    def within(self, t):
        return pl.ds(pl.multiple_of(t * self.unit, 128), self.unit)

    def enter(self, x):
        if self.direct:
            return x
        lead = x.shape[:-1]
        x = x.reshape(lead + (self.m, self.n, self.piece))
        return jnp.swapaxes(x, -3, -2).reshape(lead + (-1,))

    def leave(self, x):
        if self.direct:
            return x
        lead = x.shape[:-1]
        x = x.reshape(lead + (self.n, self.m, self.piece))
        return jnp.swapaxes(x, -3, -2).reshape(lead + (-1,))


def inverse_rms(x_ref, lay):
    tok, width = x_ref.shape

    def one(i, total):
        v = x_ref[:, pl.ds(pl.multiple_of(i * 512, 512), 512)].astype(F32)
        v = v * v
        part = v[:, :128]
        for q in range(1, 4):
            part = part + v[:, q * 128 : (q + 1) * 128]
        return total + part

    total = lax.fori_loop(0, width // 512, one, jnp.zeros((tok, 128), F32))
    return lax.rsqrt(jnp.sum(total, axis=1, keepdims=True) / width + EPSILON)


def far_first(n):
    return sorted(range(1, n), key=lambda j: -min(j, n - j))


def near_first(n):
    return sorted(range(1, n), key=lambda j: min(j, n - j))


def forward_kernel(
    lay, back,
    x_ref, gain_ref, w_ref, doc_ref,
    cols_out, slab_out, kv_ref, docs_ref,
    cols, send, slab, own, psend, precv, kvown,
    wsend, wrecv, fsend, frecv, asend, arecv, rsend, rrecv, ksend, krecv, dsend, drecv, lsem,
):
    n, m, piece = lay.n, lay.m, lay.piece
    s = lax.axis_index("seq")
    b = lax.axis_index("blk")
    partner = b + 1 - 2 * lax.rem(b, 2)
    half = m // 2
    greet(n, m)

    def rows(owner):
        return pl.ds(pl.multiple_of(owner * piece, piece), piece)

    spread = []
    for k in range(1, half):
        copy = remote(
            w_ref, slab.at[rows(b)], wsend.at[k], wrecv.at[k], blk=lax.rem(b + 2 * k, m)
        )
        copy.start()
        spread.append(copy)
    first = remote(w_ref, slab.at[rows(b)], fsend.at[0], frecv.at[0], blk=partner)
    first.start()
    mine = pltpu.make_async_copy(w_ref, slab.at[rows(b)], lsem.at[0])
    mine.start()

    doc_copies = []
    for j in range(1, back + 1):
        copy = remote(
            doc_ref, docs_ref.at[j], dsend.at[j], drecv.at[j], seq=lax.rem(s + j, n)
        )
        doc_copies.append(copy)

        @pl.when(s + j < n)
        def _(copy=copy):
            copy.start()

    inv = inverse_rms(x_ref, lay)

    def normed_into(ref, sp):
        def one(t, carry):
            v = x_ref[:, lay.cols(sp, t)].astype(F32) * inv
            g = gain_ref[pl.ds(lay.row(sp, t), 1), :]
            ref[:, lay.within(t)] = (v * g).astype(BF16)
            return carry

        lax.fori_loop(0, lay.units, one, 0)

    out_copies = []
    for j in far_first(n):
        sp = lax.rem(s + j, n)
        normed_into(send.at[j - 1], sp)
        copy = remote(send.at[j - 1], cols.at[s], asend.at[j], arecv.at[j], seq=sp)
        copy.start()
        out_copies.append(copy)
    normed_into(cols.at[s], s)
    docs_ref[0] = doc_ref[...]
    for j in range(1, back + 1):

        @pl.when(s - j < 0)
        def _(j=j):
            docs_ref[j] = jnp.full(docs_ref.shape[1:], -1, jnp.int32)
            kv_ref[j] = jnp.zeros(kv_ref.shape[1:], BF16)

    mine.wait()
    forwards = []
    for k in range(1, half):
        spread[k - 1].wait_recv()
        shard = slab.at[rows(lax.rem(b - 2 * k + m, m))]
        copy = remote(shard, shard, fsend.at[k], frecv.at[k], blk=partner)
        copy.start()
        forwards.append(copy)
    first.wait_recv()
    for copy in forwards:
        copy.wait_recv()
    keep = [pltpu.make_async_copy(slab, slab_out, lsem.at[0])]
    keep[0].start()

    def project(source, target):
        def one(c, carry):
            at = pl.ds(pl.multiple_of(c * 256, 256), 256)
            target[:, at] = jnp.dot(
                cols[source], slab[:, at], preferred_element_type=F32
            )
            return carry

        lax.fori_loop(0, target.shape[1] // 256, one, 0)

    sums = []
    for j in near_first(n):
        source = lax.rem(s - j + n, n)
        remote(send.at[j - 1], cols.at[source], asend.at[j], arecv.at[j], seq=source).wait_recv()
        project(source, psend.at[j - 1])
        copy = remote(
            psend.at[j - 1], precv.at[j - 1], rsend.at[j], rrecv.at[j], seq=source
        )
        copy.start()
        sums.append(copy)
    keep.append(pltpu.make_async_copy(cols, cols_out, lsem.at[1]))
    keep[1].start()
    project(s, own)
    for copy in sums:
        copy.wait_recv()

    def add_up(c, carry):
        at = pl.ds(pl.multiple_of(c * 256, 256), 256)
        total = own[:, at]
        for j in range(1, n):
            total = total + precv[j - 1, :, at]
        kvown[:, at] = total.astype(BF16)
        return carry

    lax.fori_loop(0, own.shape[1] // 256, add_up, 0)
    kv_copies = []
    for j in range(1, back + 1):
        copy = remote(kvown, kv_ref.at[j], ksend.at[j], krecv.at[j], seq=lax.rem(s + j, n))
        kv_copies.append(copy)

        @pl.when(s + j < n)
        def _(copy=copy):
            copy.start()

    kv_ref[0] = kvown[...]
    for j in range(1, back + 1):

        @pl.when(s - j >= 0)
        def _(j=j):
            kv_copies[j - 1].wait_recv()
            doc_copies[j - 1].wait_recv()

        @pl.when(s + j < n)
        def _(j=j):
            kv_copies[j - 1].wait_send()
            doc_copies[j - 1].wait_send()

    for copy in spread + [first] + forwards + out_copies + sums:
        copy.wait_send()
    for copy in keep:
        copy.wait()


def run_forward(lay, back, x, gain, w, docs):
    n, m, piece = lay.n, lay.m, lay.piece
    tok, kvc = x.shape[0], w.shape[1]
    dma = pltpu.SemaphoreType.DMA
    vmem = pl.BlockSpec(memory_space=pltpu.VMEM)
    hbm = pl.BlockSpec(memory_space=pl.ANY)
    return pl.pallas_call(
        functools.partial(forward_kernel, lay, back),
        name="forward_exchange",
        out_shape=(
            jax.ShapeDtypeStruct((n, tok, lay.wide), BF16),
            jax.ShapeDtypeStruct((lay.wide, kvc), BF16),
            jax.ShapeDtypeStruct((back + 1, tok, kvc), BF16),
            jax.ShapeDtypeStruct((back + 1,) + docs.shape, jnp.int32),
        ),
        in_specs=[vmem] * 4,
        out_specs=(hbm, hbm, vmem, vmem),
        scratch_shapes=[
            pltpu.VMEM((n, tok, lay.wide), BF16),
            pltpu.VMEM((n - 1, tok, lay.wide), BF16),
            pltpu.VMEM((lay.wide, kvc), BF16),
            pltpu.VMEM((tok, kvc), F32),
            pltpu.VMEM((n - 1, tok, kvc), F32),
            pltpu.VMEM((n - 1, tok, kvc), F32),
            pltpu.VMEM((tok, kvc), BF16),
            dma((m // 2,)), dma((m // 2,)), dma((m // 2,)), dma((m // 2,)),
            dma((n,)), dma((n,)), dma((n,)), dma((n,)),
            dma((n,)), dma((n,)), dma((n,)), dma((n,)),
            dma((2,)),
        ],
        compiler_params=pltpu.CompilerParams(
            collective_id=0, has_side_effects=True, vmem_limit_bytes=VMEM_LIMIT
        ),
    )(x, gain, w, docs)


def attention_kernel(
    group, q_ref, g_ref, k_ref, v_ref, docs_ref, doc_ref, att_ref, dq_ref, own_ref, far_ref, dk, dv
):
    slots, tok = k_ref.shape[0], k_ref.shape[1]
    keys = slots * tok
    scale = HEAD ** (-0.5)
    k = k_ref[...].reshape(keys, HEAD)
    v = v_ref[...].reshape(keys, HEAD)
    row = lax.broadcasted_iota(jnp.int32, (tok, tok), 0)
    col = lax.broadcasted_iota(jnp.int32, (tok, tok), 1)
    mine = doc_ref[...]
    parts = [(docs_ref[0, 0:1, :] == mine) & (col <= row)]
    for j in range(1, slots):
        parts.append(docs_ref[j, 0:1, :] == mine)
    bias = jnp.concatenate([jnp.where(p, 1.0, 0.0).astype(F32) for p in parts], axis=1)
    allowed = bias > 0.5
    dk[...] = jnp.zeros_like(dk)
    dv[...] = jnp.zeros_like(dv)
    nt = (((1,), (1,)), ((), ()))
    tn = (((0,), (0,)), ((), ()))

    def head(h, carry):
        at = pl.ds(pl.multiple_of(h * HEAD, HEAD), HEAD)
        q = q_ref[:, at]
        g = g_ref[:, at]
        raw = lax.dot_general(q, k, nt, preferred_element_type=F32) * scale
        masked = jnp.where(allowed, raw, -1e30)
        top = jnp.max(masked, axis=1, keepdims=True)
        expo = jnp.where(allowed, jnp.exp(masked - top), 0.0)
        inv = 1.0 / jnp.sum(expo, axis=1, keepdims=True)
        att = (
            jnp.dot(expo.astype(BF16), v, preferred_element_type=F32) * inv
        ).astype(BF16)
        att_ref[:, at] = att
        delta = jnp.sum(g.astype(F32) * att.astype(F32), axis=1, keepdims=True)
        probs = expo * inv
        gp = lax.dot_general(g, v, nt, preferred_element_type=F32)
        ds = (probs * (gp - delta)).astype(BF16)
        dv[...] += lax.dot_general(probs.astype(BF16), g, tn, preferred_element_type=F32)
        dk[...] += lax.dot_general(ds, q, tn, preferred_element_type=F32)
        dq_ref[:, at] = (
            jnp.dot(ds, k, preferred_element_type=F32) * scale
        ).astype(BF16)
        return carry

    lax.fori_loop(0, group, head, 0, unroll=2)
    own_ref[0] = dk[0:tok, :] * scale
    own_ref[1] = dv[0:tok, :]
    for j in range(1, slots):
        far_ref[j - 1, 0] = (dk[j * tok : (j + 1) * tok, :] * scale).astype(BF16)
        far_ref[j - 1, 1] = dv[j * tok : (j + 1) * tok, :].astype(BF16)


def run_attention(q, g, kv, docs, doc_col):
    slots, tok, kvc = kv.shape
    heads = kvc // 2 // HEAD
    group = q.shape[1] // HEAD // heads
    gw = group * HEAD
    wide = pl.BlockSpec((tok, gw), lambda i: (0, i))
    return pl.pallas_call(
        functools.partial(attention_kernel, group),
        name="attention",
        grid=(heads,),
        out_shape=(
            jax.ShapeDtypeStruct(q.shape, BF16),
            jax.ShapeDtypeStruct(q.shape, BF16),
            jax.ShapeDtypeStruct((2, tok, kvc // 2), F32),
            jax.ShapeDtypeStruct((slots - 1, 2, tok, kvc // 2), BF16),
        ),
        in_specs=[
            wide,
            wide,
            pl.BlockSpec((slots, tok, HEAD), lambda i: (0, 0, i)),
            pl.BlockSpec((slots, tok, HEAD), lambda i: (0, 0, i + heads)),
            pl.BlockSpec(docs.shape, lambda i: (0, 0, 0)),
            pl.BlockSpec(doc_col.shape, lambda i: (0, 0)),
        ],
        out_specs=(
            wide,
            wide,
            pl.BlockSpec((2, tok, HEAD), lambda i: (0, 0, i)),
            pl.BlockSpec((slots - 1, 2, tok, HEAD), lambda i: (0, 0, 0, i)),
        ),
        scratch_shapes=[
            pltpu.VMEM((slots * tok, HEAD), F32),
            pltpu.VMEM((slots * tok, HEAD), F32),
        ],
    )(q, g, kv, kv, docs, doc_col)


def backward_kernel(
    lay, back,
    x_ref, gain_ref, cols_in, slab_in, own_ref, far_ref,
    dx_ref, dw_ref, dgain_ref,
    cols, slab, frecv_buf, gkv, nsend, nrecv, pair_send, pair_recv, keep, osend, orecv, seq_gain, blk_gain,
    psend, precv, gsend, grecv, asend, arecv, csend, crecv, wsend, wrecv, ssend, srecv, bsend, brecv, lsem,
):
    n, m, piece = lay.n, lay.m, lay.piece
    s = lax.axis_index("seq")
    b = lax.axis_index("blk")
    core = lax.rem(b, 2)
    partner = b + 1 - 2 * core
    half = m // 2
    tok, width = x_ref.shape
    kvw = own_ref.shape[2]
    loads = [
        pltpu.make_async_copy(slab_in, slab, lsem.at[0]),
        pltpu.make_async_copy(cols_in, cols, lsem.at[1]),
    ]
    for copy in loads:
        copy.start()
    greet(n, m)
    far_copies = []
    for j in range(1, back + 1):
        copy = remote(
            far_ref.at[j - 1], frecv_buf.at[j - 1], psend.at[j], precv.at[j],
            seq=lax.rem(s - j + n, n),
        )
        far_copies.append(copy)

        @pl.when(s - j >= 0)
        def _(copy=copy):
            copy.start()

        @pl.when(s + j >= n)
        def _(j=j):
            frecv_buf[j - 1] = jnp.zeros(frecv_buf.shape[1:], BF16)

    inv = inverse_rms(x_ref, lay)
    for j in range(1, back + 1):

        @pl.when(s + j < n)
        def _(j=j):
            far_copies[j - 1].wait_recv()

    for part in range(2):
        total = own_ref[part]
        for j in range(1, back + 1):
            total = total + frecv_buf[j - 1, part].astype(F32)
        gkv[s, :, part * kvw : (part + 1) * kvw] = total.astype(BF16)
    gather = []
    for j in far_first(n):
        copy = remote(
            gkv.at[s], gkv.at[s], gsend.at[j], grecv.at[j], seq=lax.rem(s + j, n)
        )
        copy.start()
        gather.append(copy)
    loads[0].wait()

    def to_normed(source, ref):
        def one(t, carry):
            rows = pl.ds(pl.multiple_of(t * lay.unit, lay.unit), lay.unit)
            ref[:, lay.within(t)] = lax.dot_general(
                gkv[source], slab[rows, :], (((1,), (1,)), ((), ())),
                preferred_element_type=F32,
            ).astype(BF16)
            return carry

        lax.fori_loop(0, lay.units, one, 0)

    to_normed(s, nrecv.at[s])
    normed_copies = []
    for j in near_first(n):
        source = lax.rem(s - j + n, n)
        remote(gkv.at[s], gkv.at[source], gsend.at[j], grecv.at[j], seq=source).wait_recv()
        to_normed(source, nsend.at[j - 1])
        copy = remote(nsend.at[j - 1], nrecv.at[s], asend.at[j], arecv.at[j], seq=source)
        copy.start()
        normed_copies.append(copy)
    loads[1].wait()

    def weight_tile(t):
        left = cols[:, :, lay.within(t)].reshape(n * tok, lay.unit)
        return lax.dot_general(
            left, gkv[...].reshape(n * tok, 2 * kvw), (((0,), (0,)), ((), ())),
            preferred_element_type=F32,
        )

    pair_copies = [
        remote(pair_send.at[k], pair_recv.at[k], csend.at[k], crecv.at[k], blk=partner)
        for k in range(half)
    ]
    per = lay.unit // piece
    if per == 1:
        for k in range(half):
            pair_send[k] = weight_tile(2 * k + 1 - core).astype(BF16)
            pair_copies[k].start()

        def kept(k, carry):
            keep[k] = weight_tile(2 * k + core)
            return carry

        lax.fori_loop(0, half, kept, 0)
    else:

        def both(t, carry):
            tile = weight_tile(t)
            for r in range(per):
                part = tile[r * piece : (r + 1) * piece]
                k = (t * per + r) // 2

                @pl.when(core == r % 2)
                def _(part=part, k=k):
                    keep[k] = part

                @pl.when(core != r % 2)
                def _(part=part, k=k):
                    pair_send[k] = part.astype(BF16)

            return carry

        lax.fori_loop(0, lay.units, both, 0)
        for copy in pair_copies:
            copy.start()
    for copy in pair_copies:
        copy.wait_recv()
    place = b // 2
    owner_copies = []
    for k in range(1, half):
        slot = lax.rem(place + k, half)
        osend[k - 1] = (keep[slot] + pair_recv[slot].astype(F32)).astype(BF16)
        copy = remote(
            osend.at[k - 1], orecv.at[k - 1], wsend.at[k], wrecv.at[k], blk=lax.rem(b + 2 * k, m)
        )
        copy.start()
        owner_copies.append(copy)

    for j in near_first(n):
        source = lax.rem(s + j, n)
        remote(nsend.at[j - 1], nrecv.at[source], asend.at[n - j], arecv.at[n - j], seq=source).wait_recv()

    def means(i, total):
        sp = i // lay.units
        t = lax.rem(i, lay.units)
        row = pl.ds(lay.row(sp, t), 1)
        scaled = x_ref[:, lay.cols(sp, t)].astype(F32) * inv
        term = nrecv[sp, :, lay.within(t)].astype(F32) * scaled
        seq_gain[pl.ds(s, 1), row, :] = jnp.sum(term, axis=0, keepdims=True)[None]
        term = term * gain_ref[row, :]
        part = term[:, :128]
        for q in range(1, lay.unit // 128):
            part = part + term[:, q * 128 : (q + 1) * 128]
        return total + part

    total = lax.fori_loop(0, n * lay.units, means, jnp.zeros((tok, 128), F32))
    seq_copies = []
    for j in range(1, n):
        copy = remote(
            seq_gain.at[s], seq_gain.at[s], ssend.at[j], srecv.at[j], seq=lax.rem(s + j, n)
        )
        copy.start()
        seq_copies.append(copy)
    mean = jnp.sum(total, axis=1, keepdims=True) / width

    def finish(i, carry):
        sp = i // lay.units
        t = lax.rem(i, lay.units)
        scaled = x_ref[:, lay.cols(sp, t)].astype(F32) * inv
        hat = nrecv[sp, :, lay.within(t)].astype(F32) * gain_ref[pl.ds(lay.row(sp, t), 1), :]
        dx_ref[:, lay.cols(sp, t)] = (inv * (hat - scaled * mean)).astype(BF16)
        return carry

    lax.fori_loop(0, n * lay.units, finish, 0)
    for j in range(1, n):
        source = lax.rem(s - j + n, n)
        remote(
            seq_gain.at[s], seq_gain.at[source], ssend.at[j], srecv.at[j], seq=source
        ).wait_recv()
    gain_sum = seq_gain[0]
    for i in range(1, n):
        gain_sum = gain_sum + seq_gain[i]
    blk_gain[b] = gain_sum
    blk_copies = []
    for j in range(1, m):
        copy = remote(
            blk_gain.at[b], blk_gain.at[b], bsend.at[j], brecv.at[j], blk=lax.rem(b + j, m)
        )
        copy.start()
        blk_copies.append(copy)
    for copy in owner_copies:
        copy.wait_recv()

    dw = keep[place] + pair_recv[place].astype(F32)
    for k in range(1, half):
        dw = dw + orecv[k - 1].astype(F32)
    dw_ref[...] = dw
    for j in range(1, m):
        source = lax.rem(b - j + m, m)
        remote(
            blk_gain.at[b], blk_gain.at[source], bsend.at[j], brecv.at[j], blk=source
        ).wait_recv()
    gain_sum = blk_gain[0]
    for i in range(1, m):
        gain_sum = gain_sum + blk_gain[i]
    dgain_ref[...] = gain_sum
    for copy in gather + normed_copies + pair_copies + owner_copies + seq_copies + blk_copies:
        copy.wait_send()
    for j in range(1, back + 1):

        @pl.when(s - j >= 0)
        def _(j=j):
            far_copies[j - 1].wait_send()


def run_backward(lay, back, x, gain, cols, slab, own, far):
    n, m, piece = lay.n, lay.m, lay.piece
    tok, width = x.shape
    kvc = slab.shape[1]
    dma = pltpu.SemaphoreType.DMA
    vmem = pl.BlockSpec(memory_space=pltpu.VMEM)
    hbm = pl.BlockSpec(memory_space=pl.ANY)
    half = m // 2
    return pl.pallas_call(
        functools.partial(backward_kernel, lay, back),
        name="backward_exchange",
        out_shape=(
            jax.ShapeDtypeStruct((tok, width), BF16),
            jax.ShapeDtypeStruct((piece, kvc), F32),
            jax.ShapeDtypeStruct(gain.shape, F32),
        ),
        in_specs=[vmem, vmem, hbm, hbm, vmem, vmem],
        out_specs=(vmem, vmem, vmem),
        scratch_shapes=[
            pltpu.VMEM(cols.shape, BF16),
            pltpu.VMEM(slab.shape, BF16),
            pltpu.VMEM(far.shape, BF16),
            pltpu.VMEM((n, tok, kvc), BF16),
            pltpu.VMEM((n - 1, tok, lay.wide), BF16),
            pltpu.VMEM((n, tok, lay.wide), BF16),
            pltpu.VMEM((half, piece, kvc), BF16),
            pltpu.VMEM((half, piece, kvc), BF16),
            pltpu.VMEM((half, piece, kvc), F32),
            pltpu.VMEM((half - 1, piece, kvc), BF16),
            pltpu.VMEM((half - 1, piece, kvc), BF16),
            pltpu.VMEM((n,) + gain.shape, F32),
            pltpu.VMEM((m,) + gain.shape, F32),
            dma((n,)), dma((n,)), dma((n,)), dma((n,)), dma((n,)), dma((n,)),
            dma((half,)), dma((half,)), dma((half,)), dma((half,)),
            dma((n,)), dma((n,)), dma((m,)), dma((m,)),
            dma((2,)),
        ],
        compiler_params=pltpu.CompilerParams(
            collective_id=1, has_side_effects=True, vmem_limit_bytes=VMEM_LIMIT
        ),
    )(x, gain, cols, slab, own, far)


def shards(layer_input, queries, grad_out, segment_ids, kv_weight, norm_gain):
    n, m = lax.axis_size("seq"), lax.axis_size("blk")
    tok = layer_input.shape[1]
    lay = Layout(n, m, kv_weight.shape[0])
    back = max(n // 2, 1)
    x = lay.enter(layer_input[0])
    gain = lay.enter(norm_gain).reshape(-1, lay.unit)
    docs = jnp.broadcast_to(segment_ids, (8, tok))
    doc_col = jnp.broadcast_to(segment_ids[0][:, None], (tok, tok))
    cols, slab, kv, all_docs = run_forward(lay, back, x, gain, kv_weight, docs)
    attended, grad_queries, own, far = run_attention(
        queries[0], grad_out[0], kv, all_docs, doc_col
    )
    dx, dw, dgain = run_backward(lay, back, x, gain, cols, slab, own, far)
    return (
        attended[None],
        grad_queries[None],
        lay.leave(dx)[None],
        dw,
        lay.leave(dgain.reshape(-1)),
    )


def solution(mesh):
    tokens = P("blk", "seq", None)
    rows = P(("blk", "seq"), None)
    return jax.shard_map(
        shards,
        mesh=mesh,
        in_specs=(tokens, tokens, tokens, P("blk", "seq"), rows, P()),
        out_specs=(tokens, tokens, tokens, rows, P()),
        check_vma=False,
    )
```

time: 394 us -> 260 us (0.66)
  Pallas kernels: 0 us -> 250 us
  blocking collectives: 221 us -> 0 us
  waiting for transfers between devices: 39.7 us -> 0 us
  matrix products: 38.6 us -> 0 us
  local copies, waits for them, and re-layouts: 45.9 us -> 8.9 us
  other arithmetic: 20.6 us -> 0 us
  between operations: 14.2 us -> 0.67 us
  starting transfers between devices: 11.5 us -> 0 us
    pallas_call x0 -> x3, Pallas kernels: none -> 250 us  [the longest x1 114 us: run_forward(): pl.pallas_call(functools.partial(forward_kernel, lay, back), name='forwar...]
    psum x3 -> x0, blocking collectives: 186 us -> none  [the longest x1 75.7 us: shards(): kv_all = lax.psum(full_terms, 'seq').astype(jnp.bfloat16)]
    all_to_all x2 -> x0, waiting for transfers between devices: 39 us -> none  [the longest x1 30.7 us: shards(): lax.all_to_all(grad_cols, 'seq', split_axis=0, concat_axis=2, tiled=True)]
    dot_general x9 -> x0, matrix products: 38.6 us -> none  [the longest x1 7.22 us: shards(): lax.dot_general(columns, grad_kv, (((0,), (0,)), ((), ())), preferred_ele...]
    all_gather x1 -> x0, blocking collectives: 35.9 us -> none  [shards(): doc_all = lax.all_gather(query_doc, 'seq', axis=0, tiled=True)]
    convert_element_type x4 -> x0, local copies, waits for them, and re-layouts: 21.1 us -> none  [the longest x2 10.6 us: shards(): source = layer_input[0].astype(f32)]
    all_to_all x2 -> x0, starting transfers between devices: 11.4 us -> none  [the longest x1 6.48 us: shards(): lax.all_to_all(split_cols, 'seq', split_axis=2, concat_axis=0, tiled=True)]
    convert_element_type x3 -> x0, other arithmetic: 10.7 us -> none  [the longest x1 4.46 us: shards(): grad_input.astype(jnp.bfloat16)[None]]
  transfers between devices with their start and end apart: 4 -> 0, of which waited for: 2 -> 0; matrix products, arithmetic and copies ran while one was open for 16% -> 0% of each run, Pallas kernels for 0% -> 0%
where the time goes in v1:
time: 260 us; the launch traced here: 259 us
  Pallas kernels  250 us (96%)
  local copies, waits for them, and re-layouts  8.9 us (3%)
    pallas_call x1, Pallas kernels, run_forward(): pl.pallas_call(functools.partial(forward_kernel, lay, back), name='forwar...  114 us
    pallas_call x1, Pallas kernels, run_backward(): pl.pallas_call(functools.partial(backward_kernel, lay, back), name='backw...  112 us
    pallas_call x1, Pallas kernels, run_attention(): pl.pallas_call(functools.partial(attention_kernel, group), name='attentio...  23.6 us
    unnamed x7, local copies, waits for them, and re-layouts  5.55 us

profile of v1, /device:TPU:0, one launch (start us, length us, event | category | flops | bytes accessed | tf_op | source)
XLA Modules:
  0.0 259.4 jit_solution(8169989056333595787)
XLA Ops:
  0.6 0.0 copy-start.1
  0.6 1.4 reshape.17.gain_ref
  2.0 1.2 broadcast_in_dim.22.doc_ref
  3.3 114.2 %forward_exchange.1 = (bf16[4,128,2048]{2,1,0:T(8,128)(2,1)}, bf16[2048,1024]{1,0:T(8,128)(2,1)}, bf16[3,128,1024]{2,1,0:T(8,128)(2,1)}, s32[3,8,128]{2,1,0:T(8,128)}) custom-call(bf16[128,8192]{1,0:T(8,128)(2,1)} %bitcast.9, f32[32,256]{1,0:T(8,128)} %reshape.17.gain_ref, bf16[256,1024]{1,0:T(8,128)(2,1)} %w_ref.1, s32[8,128]{1,0:T(8,128)} %broadcast_in_dim.22.doc_ref), custom_call_target="tpu_custom_call" | custom-call | tf_op jit(solution)/shard_map/forward_exchange/pallas_call | solution.py:249
  117.4 0.0 copy-done.1
  117.5 0.7 broadcast_in_dim.23.doc_ref
  118.2 23.6 %attention.1 = (bf16[128,4096]{1,0:T(8,128)(2,1)}, bf16[128,4096]{1,0:T(8,128)(2,1)}, f32[2,128,512]{2,1,0:T(8,128)}, bf16[2,2,128,512]{3,2,1,0:T(8,128)(2,1)}) custom-call(bf16[128,4096]{1,0:T(8,128)(2,1)} %bitcast.12, bf16[128,4096]{1,0:T(8,128)(2,1)} %bitcast.13, bf16[3,128,1024]{2,1,0:T(8,128)(2,1)} %get-tuple-element.16.k_ref.v_ref, ...), custom_call_target="tpu_custom_call" | custom-call | tf_op jit(solution)/shard_map/attention/pallas_call | solution.py:338
  141.8 112.1 %backward_exchange.1 = (bf16[128,8192]{1,0:T(8,128)(2,1)}, f32[256,1024]{1,0:T(8,128)}, f32[32,256]{1,0:T(8,128)}) custom-call(bf16[128,8192]{1,0:T(8,128)(2,1)} %bitcast.10, f32[32,256]{1,0:T(8,128)} %reshape.17.gain_ref, bf16[4,128,2048]{2,1,0:T(8,128)(2,1)} %get-tuple-element.20.cols_in, bf16[2048,1024]{1,0:T(8,128)(2,1)} %get-tuple-element.21.slab_in, ...), custom_call_target="tpu_custom_call" | custom-call | tf_op jit(solution)/shard_map/backward_exchange/pallas_call | solution.py:591
  253.8 1.4 copy.11
  255.2 0.0 copy-start
  255.2 3.2 %copy.14 = bf16[1,128,8192]{2,1,0:T(8,128)(2,1)} copy(bf16[1,128,8192]{2,1,0:T(8,128)(2,1)} %bitcast.11) | data formatting | bytes 4194304
  258.4 0.0 copy-done
  258.4 1.0 copy.15
Async XLA Ops:
  0.6 116.8 %copy-start.1 = (s32[1,128]{1,0:T(1,128)S(1)}, s32[1,128]{1,0:T(1,128)}, u32[]{:S(2)}) copy-start(s32[1,128]{1,0:T(1,128)} %param.9) | copy-start | bytes 1540
  255.2 3.2 %copy-start = (f32[256,1024]{1,0:T(8,128)S(1)}, f32[256,1024]{1,0:T(8,128)}, u32[]{:S(2)}) copy-start(f32[256,1024]{1,0:T(8,128)} %get-tuple-element.35) | copy-start | bytes 3145732

commit v2 on v1

v2 whole, which is shorter than its diff:
```python
import functools

import jax
import jax.numpy as jnp
from jax import lax
from jax.experimental import pallas as pl
from jax.experimental.pallas import tpu as pltpu
from jax.sharding import PartitionSpec as P

HEAD = 128
EPSILON = 1e-05
F32 = jnp.float32
BF16 = jnp.bfloat16
MESH = pl.DeviceIdType.MESH
VMEM_LIMIT = 60 * 1024 * 1024


def remote(src, dst, send_sem, recv_sem, **where):
    return pltpu.make_async_remote_copy(
        src_ref=src,
        dst_ref=dst,
        send_sem=send_sem,
        recv_sem=recv_sem,
        device_id=where,
        device_id_type=MESH,
    )


def greet(n, m):
    s = lax.axis_index("seq")
    b = lax.axis_index("blk")
    barrier = pltpu.get_barrier_semaphore()
    for j in range(1, n):
        pl.semaphore_signal(
            barrier, inc=1, device_id={"seq": lax.rem(s + j, n)}, device_id_type=MESH
        )
    for j in range(1, m):
        pl.semaphore_signal(
            barrier, inc=1, device_id={"blk": lax.rem(b + j, m)}, device_id_type=MESH
        )
    pl.semaphore_wait(barrier, n - 1 + m - 1)


def inverse_rms(x_ref):
    tok, width = x_ref.shape

    def one(i, total):
        v = x_ref[:, pl.ds(pl.multiple_of(i * 512, 512), 512)].astype(F32)
        v = v * v
        part = v[:, :128]
        for q in range(1, 4):
            part = part + v[:, q * 128 : (q + 1) * 128]
        return total + part

    total = lax.fori_loop(0, width // 512, one, jnp.zeros((tok, 128), F32))
    return lax.rsqrt(jnp.sum(total, axis=1, keepdims=True) / width + EPSILON)


def far_first(n):
    return sorted(range(1, n), key=lambda j: -min(j, n - j))


def lanes(i, size):
    return pl.ds(pl.multiple_of(i * size, 128), size)


def forward_kernel(
    n, m, back,
    x_ref, gain_ref, w_ref, doc_ref,
    cols_out, slab_out, kv_ref, docs_ref,
    cols, send, slab, own, psend, precv,
    usend, urecv, dsend, drecv, fsend, frecv, asend, arecv, rsend, rrecv, ksend, krecv, osend, orecv, lsem,
):
    piece = w_ref.shape[0]
    wide = cols.shape[2]
    half = m // 2
    s = lax.axis_index("seq")
    b = lax.axis_index("blk")
    core = lax.rem(b, 2)
    chip = b // 2
    partner = b + 1 - 2 * core
    greet(n, m)

    def rows(of_core, of_seq):
        return pl.ds(pl.multiple_of((of_core * n + of_seq) * piece, piece), piece)

    up, down = lax.rem(s + 1, n), lax.rem(s + n - 1, n)
    own_rows = rows(core, s)
    first = remote(w_ref, slab.at[own_rows], fsend.at[0], frecv.at[0], blk=partner)

    def hop(source, sender, sems, i, target):
        at = rows(core, source)
        return remote(slab.at[at] if i else w_ref, slab.at[at], sems[0].at[i], sems[1].at[i], seq=target)

    going_up = [hop(lax.rem(s - i + n, n), s, (usend, urecv), i, up) for i in range(n - 1)]
    going_down = [hop(lax.rem(s + i, n), s, (dsend, drecv), i, down) for i in range(n - 1)]

    @pl.when(s + 1 < n)
    def _():
        going_up[0].start()

    @pl.when(s >= 1)
    def _():
        going_down[0].start()

    first.start()
    mine = pltpu.make_async_copy(w_ref, slab.at[own_rows], lsem.at[0])
    mine.start()

    doc_copies = []
    for j in range(1, back + 1):
        copy = remote(
            doc_ref, docs_ref.at[j], osend.at[j], orecv.at[j], seq=lax.rem(s + j, n)
        )
        doc_copies.append(copy)

        @pl.when(s + j < n)
        def _(copy=copy):
            copy.start()

    inv = inverse_rms(x_ref)
    per = wide // 512

    def normed_into(ref, of_chip):
        def one(t, carry):
            at = lanes(of_chip * per + t, 512)
            v = x_ref[:, at].astype(F32) * inv
            ref[:, lanes(t, 512)] = (v * gain_ref[:, at]).astype(BF16)
            return carry

        lax.fori_loop(0, per, one, 0)

    out_copies = []
    for k in range(1, half):
        normed_into(send.at[k - 1], lax.rem(chip + k, half))
        copy = remote(
            send.at[k - 1], cols.at[chip], asend.at[k], arecv.at[k], blk=lax.rem(b + 2 * k, m)
        )
        copy.start()
        out_copies.append(copy)
    normed_into(cols.at[chip], chip)
    docs_ref[0] = doc_ref[...]
    for j in range(1, back + 1):

        @pl.when(s - j < 0)
        def _(j=j):
            docs_ref[j] = jnp.full(docs_ref.shape[1:], -1, jnp.int32)
            kv_ref[j] = jnp.zeros(kv_ref.shape[1:], BF16)

    mine.wait()
    to_partner = []
    for i in range(1, n):
        for side, sems, chain, at_edge in (
            (-1, (usend, urecv), going_up, s - i >= 0),
            (1, (dsend, drecv), going_down, s + i < n),
        ):
            source = lax.rem(s + side * i + n, n)
            slot = i if side < 0 else n - 1 + i
            shard = slab.at[rows(core, source)]
            copy = remote(shard, shard, fsend.at[slot], frecv.at[slot], blk=partner)
            to_partner.append((copy, at_edge))
            more = (s + 1 < n) if side < 0 else (s >= 1)

            @pl.when(at_edge)
            def _(copy=copy, sems=sems, chain=chain, shard=shard, i=i, more=more, side=side):
                remote(
                    shard, shard, sems[0].at[i - 1], sems[1].at[i - 1], seq=up if side < 0 else down
                ).wait_recv()
                if i < n - 1:

                    @pl.when(more)
                    def _():
                        chain[i].start()

                copy.start()

    first.wait_recv()
    for copy, there in to_partner:

        @pl.when(there)
        def _(copy=copy):
            copy.wait_recv()

    keep = [pltpu.make_async_copy(slab, slab_out, lsem.at[0])]
    keep[0].start()

    def project(source, target):
        def one(t, carry):
            at = lanes(t, 256)
            target[:, at] = jnp.dot(cols[source], slab[:, at], preferred_element_type=F32)
            return carry

        lax.fori_loop(0, target.shape[1] // 256, one, 0)

    sums = []
    for k in range(1, half):
        source = lax.rem(chip - k + half, half)
        back_to = lax.rem(b - 2 * k + m, m)
        remote(send.at[k - 1], cols.at[source], asend.at[k], arecv.at[k], blk=back_to).wait_recv()
        project(source, psend.at[k - 1])
        copy = remote(psend.at[k - 1], precv.at[k - 1], rsend.at[k], rrecv.at[k], blk=back_to)
        copy.start()
        sums.append(copy)
    keep.append(pltpu.make_async_copy(cols, cols_out, lsem.at[1]))
    keep[1].start()
    project(chip, own)
    for copy in sums:
        copy.wait_recv()

    def add_up(t, carry):
        at = lanes(t, 256)
        total = own[:, at]
        for k in range(1, half):
            total = total + precv[k - 1, :, at]
        kv_ref[0, :, at] = total.astype(BF16)
        return carry

    lax.fori_loop(0, own.shape[1] // 256, add_up, 0)
    kv_copies = [
        remote(kv_ref.at[j], kv_ref.at[j + 1], ksend.at[j], krecv.at[j], seq=up)
        for j in range(back)
    ]
    for j in range(back):
        if j:

            @pl.when(s - j >= 0)
            def _(j=j):
                kv_copies[j - 1].wait_recv()

        @pl.when((s - j >= 0) & (s + 1 < n))
        def _(j=j):
            kv_copies[j].start()

    @pl.when(s - back >= 0)
    def _():
        kv_copies[back - 1].wait_recv()

    for j in range(back):

        @pl.when((s - j >= 0) & (s + 1 < n))
        def _(j=j):
            kv_copies[j].wait_send()

    for j in range(1, back + 1):

        @pl.when(s - j >= 0)
        def _(j=j):
            doc_copies[j - 1].wait_recv()

        @pl.when(s + j < n)
        def _(j=j):
            doc_copies[j - 1].wait_send()

    for i in range(n - 1):

        @pl.when((s - i >= 0) & (s + 1 < n))
        def _(i=i):
            going_up[i].wait_send()

        @pl.when((s + i < n) & (s >= 1))
        def _(i=i):
            going_down[i].wait_send()

    for copy, there in to_partner:

        @pl.when(there)
        def _(copy=copy):
            copy.wait_send()

    for copy in [first] + out_copies + sums:
        copy.wait_send()
    for copy in keep:
        copy.wait()


def run_forward(n, m, back, x, gain, w, docs):
    tok, width = x.shape
    piece, kvc = w.shape
    half = m // 2
    wide = width // half
    dma = pltpu.SemaphoreType.DMA
    vmem = pl.BlockSpec(memory_space=pltpu.VMEM)
    hbm = pl.BlockSpec(memory_space=pl.ANY)
    return pl.pallas_call(
        functools.partial(forward_kernel, n, m, back),
        name="forward_exchange",
        out_shape=(
            jax.ShapeDtypeStruct((half, tok, wide), BF16),
            jax.ShapeDtypeStruct((wide, kvc), BF16),
            jax.ShapeDtypeStruct((back + 1, tok, kvc), BF16),
            jax.ShapeDtypeStruct((back + 1,) + docs.shape, jnp.int32),
        ),
        in_specs=[vmem] * 4,
        out_specs=(hbm, hbm, vmem, vmem),
        scratch_shapes=[
            pltpu.VMEM((half, tok, wide), BF16),
            pltpu.VMEM((half - 1, tok, wide), BF16),
            pltpu.VMEM((wide, kvc), BF16),
            pltpu.VMEM((tok, kvc), F32),
            pltpu.VMEM((half - 1, tok, kvc), F32),
            pltpu.VMEM((half - 1, tok, kvc), F32),
            dma((n,)), dma((n,)), dma((n,)), dma((n,)),
            dma((2 * n,)), dma((2 * n,)),
            dma((half,)), dma((half,)), dma((half,)), dma((half,)),
            dma((n,)), dma((n,)), dma((n,)), dma((n,)),
            dma((2,)),
        ],
        compiler_params=pltpu.CompilerParams(
            collective_id=0, has_side_effects=True, vmem_limit_bytes=VMEM_LIMIT
        ),
    )(x, gain, w, docs)


def attention_kernel(
    group, q_ref, g_ref, k_ref, v_ref, docs_ref, doc_ref, att_ref, dq_ref, own_ref, far_ref, dk, dv
):
    slots, tok = k_ref.shape[0], k_ref.shape[1]
    keys = slots * tok
    scale = HEAD ** (-0.5)
    k = k_ref[...].reshape(keys, HEAD)
    v = v_ref[...].reshape(keys, HEAD)
    row = lax.broadcasted_iota(jnp.int32, (tok, tok), 0)
    col = lax.broadcasted_iota(jnp.int32, (tok, tok), 1)
    mine = doc_ref[...]
    parts = [(docs_ref[0, 0:1, :] == mine) & (col <= row)]
    for j in range(1, slots):
        parts.append(docs_ref[j, 0:1, :] == mine)
    bias = jnp.concatenate([jnp.where(p, 1.0, 0.0).astype(F32) for p in parts], axis=1)
    allowed = bias > 0.5
    dk[...] = jnp.zeros_like(dk)
    dv[...] = jnp.zeros_like(dv)
    nt = (((1,), (1,)), ((), ()))
    tn = (((0,), (0,)), ((), ()))

    def head(h, carry):
        at = pl.ds(pl.multiple_of(h * HEAD, HEAD), HEAD)
        q = q_ref[:, at]
        g = g_ref[:, at]
        raw = lax.dot_general(q, k, nt, preferred_element_type=F32) * scale
        masked = jnp.where(allowed, raw, -1e30)
        top = jnp.max(masked, axis=1, keepdims=True)
        expo = jnp.where(allowed, jnp.exp(masked - top), 0.0)
        inv = 1.0 / jnp.sum(expo, axis=1, keepdims=True)
        att = (
            jnp.dot(expo.astype(BF16), v, preferred_element_type=F32) * inv
        ).astype(BF16)
        att_ref[:, at] = att
        delta = jnp.sum(g.astype(F32) * att.astype(F32), axis=1, keepdims=True)
        probs = expo * inv
        gp = lax.dot_general(g, v, nt, preferred_element_type=F32)
        ds = (probs * (gp - delta)).astype(BF16)
        dv[...] += lax.dot_general(probs.astype(BF16), g, tn, preferred_element_type=F32)
        dk[...] += lax.dot_general(ds, q, tn, preferred_element_type=F32)
        dq_ref[:, at] = (
            jnp.dot(ds, k, preferred_element_type=F32) * scale
        ).astype(BF16)
        return carry

    lax.fori_loop(0, group, head, 0, unroll=2)
    own_ref[0] = dk[0:tok, :] * scale
    own_ref[1] = dv[0:tok, :]
    for j in range(1, slots):
        far_ref[j - 1, 0] = (dk[j * tok : (j + 1) * tok, :] * scale).astype(BF16)
        far_ref[j - 1, 1] = dv[j * tok : (j + 1) * tok, :].astype(BF16)


def run_attention(q, g, kv, docs, doc_col):
    slots, tok, kvc = kv.shape
    heads = kvc // 2 // HEAD
    group = q.shape[1] // HEAD // heads
    gw = group * HEAD
    wide = pl.BlockSpec((tok, gw), lambda i: (0, i))
    return pl.pallas_call(
        functools.partial(attention_kernel, group),
        name="attention",
        grid=(heads,),
        out_shape=(
            jax.ShapeDtypeStruct(q.shape, BF16),
            jax.ShapeDtypeStruct(q.shape, BF16),
            jax.ShapeDtypeStruct((2, tok, kvc // 2), F32),
            jax.ShapeDtypeStruct((slots - 1, 2, tok, kvc // 2), BF16),
        ),
        in_specs=[
            wide,
            wide,
            pl.BlockSpec((slots, tok, HEAD), lambda i: (0, 0, i)),
            pl.BlockSpec((slots, tok, HEAD), lambda i: (0, 0, i + heads)),
            pl.BlockSpec(docs.shape, lambda i: (0, 0, 0)),
            pl.BlockSpec(doc_col.shape, lambda i: (0, 0)),
        ],
        out_specs=(
            wide,
            wide,
            pl.BlockSpec((2, tok, HEAD), lambda i: (0, 0, i)),
            pl.BlockSpec((slots - 1, 2, tok, HEAD), lambda i: (0, 0, 0, i)),
        ),
        scratch_shapes=[
            pltpu.VMEM((slots * tok, HEAD), F32),
            pltpu.VMEM((slots * tok, HEAD), F32),
        ],
    )(q, g, kv, kv, docs, doc_col)


def backward_kernel(
    n, m, back,
    x_ref, gain_ref, cols_in, slab_in, own_ref, far_ref,
    dx_ref, dw_ref, dgain_ref,
    cols, slab, far_buf, gkv, nsend, nrecv, pair_send, pair_recv, keep, osend, orecv, seq_gain, blk_gain,
    psend, precv, gsend, grecv, asend, arecv, csend, crecv, wsend, wrecv, ssend, srecv, bsend, brecv, lsem,
):
    piece = dw_ref.shape[0]
    wide = cols.shape[2]
    half = m // 2
    s = lax.axis_index("seq")
    b = lax.axis_index("blk")
    core = lax.rem(b, 2)
    chip = b // 2
    partner = b + 1 - 2 * core
    tok, width = x_ref.shape
    kvw = own_ref.shape[2]
    loads = [
        pltpu.make_async_copy(cols_in, cols, lsem.at[0]),
        pltpu.make_async_copy(slab_in, slab, lsem.at[1]),
    ]
    for copy in loads:
        copy.start()
    greet(n, m)
    far_copies = []
    for j in range(1, back + 1):
        copy = remote(
            far_ref.at[j - 1], far_buf.at[j - 1], psend.at[j], precv.at[j],
            seq=lax.rem(s - j + n, n),
        )
        far_copies.append(copy)

        @pl.when(s - j >= 0)
        def _(copy=copy):
            copy.start()

        @pl.when(s + j >= n)
        def _(j=j):
            far_buf[j - 1] = jnp.zeros(far_buf.shape[1:], BF16)

    inv = inverse_rms(x_ref)
    for j in range(1, back + 1):

        @pl.when(s + j < n)
        def _(j=j):
            far_copies[j - 1].wait_recv()

    for part in range(2):
        total = own_ref[part]
        for j in range(1, back + 1):
            total = total + far_buf[j - 1, part].astype(F32)
        gkv[chip, :, part * kvw : (part + 1) * kvw] = total.astype(BF16)
    gather = []
    for k in range(1, half):
        copy = remote(
            gkv.at[chip], gkv.at[chip], gsend.at[k], grecv.at[k], blk=lax.rem(b + 2 * k, m)
        )
        copy.start()
        gather.append(copy)
    for copy in loads:
        copy.wait()

    def to_normed(source, ref):
        def one(t, carry):
            rows = pl.ds(pl.multiple_of(t * 256, 256), 256)
            ref[:, lanes(t, 256)] = lax.dot_general(
                gkv[source], slab[rows, :], (((1,), (1,)), ((), ())),
                preferred_element_type=F32,
            ).astype(BF16)
            return carry

        lax.fori_loop(0, wide // 256, one, 0)

    to_normed(chip, nrecv.at[chip])
    for k in range(1, half):
        source = lax.rem(chip - k + half, half)
        remote(
            gkv.at[chip], gkv.at[source], gsend.at[k], grecv.at[k], blk=lax.rem(b - 2 * k + m, m)
        ).wait_recv()

    tile = 256
    tiles = n * piece // tile

    def weight_tile(of_core, t):
        left = cols[:, :, lanes(of_core * tiles + t, tile)].reshape(half * tok, tile)
        return lax.dot_general(
            left, gkv[...].reshape(half * tok, 2 * kvw), (((0,), (0,)), ((), ())),
            preferred_element_type=F32,
        )

    pair_copies = []
    for t in range(tiles):
        at = pl.ds(t * tile, tile)
        pair_send[at] = weight_tile(1 - core, t).astype(BF16)
        copy = remote(pair_send.at[at], pair_recv.at[at], csend.at[t], crecv.at[t], blk=partner)
        copy.start()
        pair_copies.append(copy)

    def kept(t, carry):
        keep[pl.ds(pl.multiple_of(t * tile, tile), tile)] = weight_tile(core, t)
        return carry

    lax.fori_loop(0, tiles, kept, 0)
    for copy in pair_copies:
        copy.wait_recv()
    owner_copies = []
    for j in far_first(n):
        target = lax.rem(s + j, n)
        at = pl.ds(pl.multiple_of(target * piece, piece), piece)
        osend[j - 1] = (keep[at] + pair_recv[at].astype(F32)).astype(BF16)
        copy = remote(osend.at[j - 1], orecv.at[j - 1], wsend.at[j], wrecv.at[j], seq=target)
        copy.start()
        owner_copies.append(copy)

    normed_copies = []
    for k in range(1, half):
        source = lax.rem(chip - k + half, half)
        to_normed(source, nsend.at[k - 1])
        copy = remote(
            nsend.at[k - 1], nrecv.at[chip], asend.at[k], arecv.at[k], blk=lax.rem(b - 2 * k + m, m)
        )
        copy.start()
        normed_copies.append(copy)

    for k in range(1, half):
        source = lax.rem(chip + k, half)
        remote(
            nsend.at[k - 1], nrecv.at[source], asend.at[k], arecv.at[k], blk=lax.rem(b + 2 * k, m)
        ).wait_recv()

    per = wide // 256

    def means(i, total):
        at = lanes(i, 256)
        scaled = x_ref[:, at].astype(F32) * inv
        term = nrecv[i // per, :, lanes(lax.rem(i, per), 256)].astype(F32) * scaled
        seq_gain[s, pl.ds(i, 1), :] = jnp.sum(term, axis=0, keepdims=True)
        term = term * gain_ref[:, at]
        return total + term[:, :128] + term[:, 128:]

    total = lax.fori_loop(0, width // 256, means, jnp.zeros((tok, 128), F32))
    seq_copies = []
    for j in range(1, n):
        copy = remote(
            seq_gain.at[s], seq_gain.at[s], ssend.at[j], srecv.at[j], seq=lax.rem(s + j, n)
        )
        copy.start()
        seq_copies.append(copy)
    mean = jnp.sum(total, axis=1, keepdims=True) / width

    def finish(i, carry):
        at = lanes(i, 256)
        scaled = x_ref[:, at].astype(F32) * inv
        hat = nrecv[i // per, :, lanes(lax.rem(i, per), 256)].astype(F32) * gain_ref[:, at]
        dx_ref[:, at] = (inv * (hat - scaled * mean)).astype(BF16)
        return carry

    lax.fori_loop(0, width // 256, finish, 0)
    for j in range(1, n):
        source = lax.rem(s - j + n, n)
        remote(
            seq_gain.at[s], seq_gain.at[source], ssend.at[j], srecv.at[j], seq=source
        ).wait_recv()
    gain_sum = seq_gain[0]
    for i in range(1, n):
        gain_sum = gain_sum + seq_gain[i]
    blk_gain[b] = gain_sum
    blk_copies = []
    for j in range(1, m):
        copy = remote(
            blk_gain.at[b], blk_gain.at[b], bsend.at[j], brecv.at[j], blk=lax.rem(b + j, m)
        )
        copy.start()
        blk_copies.append(copy)
    for copy in owner_copies:
        copy.wait_recv()

    at = pl.ds(pl.multiple_of(s * piece, piece), piece)
    dw = keep[at] + pair_recv[at].astype(F32)
    for j in range(1, n):
        dw = dw + orecv[j - 1].astype(F32)
    dw_ref[...] = dw
    for j in range(1, m):
        source = lax.rem(b - j + m, m)
        remote(
            blk_gain.at[b], blk_gain.at[source], bsend.at[j], brecv.at[j], blk=source
        ).wait_recv()
    gain_sum = blk_gain[0]
    for i in range(1, m):
        gain_sum = gain_sum + blk_gain[i]
    dgain_ref[...] = gain_sum
    for copy in gather + normed_copies + pair_copies + owner_copies + seq_copies + blk_copies:
        copy.wait_send()
    for j in range(1, back + 1):

        @pl.when(s - j >= 0)
        def _(j=j):
            far_copies[j - 1].wait_send()


def run_backward(n, m, back, piece, x, gain, cols, slab, own, far):
    tok, width = x.shape
    wide, kvc = slab.shape
    dma = pltpu.SemaphoreType.DMA
    vmem = pl.BlockSpec(memory_space=pltpu.VMEM)
    hbm = pl.BlockSpec(memory_space=pl.ANY)
    half = m // 2
    gains = (width // 256, 256)
    return pl.pallas_call(
        functools.partial(backward_kernel, n, m, back),
        name="backward_exchange",
        out_shape=(
            jax.ShapeDtypeStruct((tok, width), BF16),
            jax.ShapeDtypeStruct((piece, kvc), F32),
            jax.ShapeDtypeStruct(gains, F32),
        ),
        in_specs=[vmem, vmem, hbm, hbm, vmem, vmem],
        out_specs=(vmem, vmem, vmem),
        scratch_shapes=[
            pltpu.VMEM(cols.shape, BF16),
            pltpu.VMEM(slab.shape, BF16),
            pltpu.VMEM(far.shape, BF16),
            pltpu.VMEM((half, tok, kvc), BF16),
            pltpu.VMEM((half - 1, tok, wide), BF16),
            pltpu.VMEM((half, tok, wide), BF16),
            pltpu.VMEM((n * piece, kvc), BF16),
            pltpu.VMEM((n * piece, kvc), BF16),
            pltpu.VMEM((n * piece, kvc), F32),
            pltpu.VMEM((n - 1, piece, kvc), BF16),
            pltpu.VMEM((n - 1, piece, kvc), BF16),
            pltpu.VMEM((n,) + gains, F32),
            pltpu.VMEM((m,) + gains, F32),
            dma((n,)), dma((n,)), dma((half,)), dma((half,)), dma((half,)), dma((half,)),
            dma((n,)), dma((n,)), dma((n,)), dma((n,)),
            dma((n,)), dma((n,)), dma((m,)), dma((m,)),
            dma((2,)),
        ],
        compiler_params=pltpu.CompilerParams(
            collective_id=1, has_side_effects=True, vmem_limit_bytes=VMEM_LIMIT
        ),
    )(x, gain, cols, slab, own, far)


def shards(layer_input, queries, grad_out, segment_ids, kv_weight, norm_gain):
    n, m = lax.axis_size("seq"), lax.axis_size("blk")
    tok = layer_input.shape[1]
    back = max(n // 2, 1)
    x = layer_input[0]
    gain = norm_gain[None]
    docs = jnp.broadcast_to(segment_ids, (8, tok))
    doc_col = jnp.broadcast_to(segment_ids[0][:, None], (tok, tok))
    cols, slab, kv, all_docs = run_forward(n, m, back, x, gain, kv_weight, docs)
    attended, grad_queries, own, far = run_attention(
        queries[0], grad_out[0], kv, all_docs, doc_col
    )
    dx, dw, dgain = run_backward(
        n, m, back, kv_weight.shape[0], x, gain, cols, slab, own, far
    )
    return attended[None], grad_queries[None], dx[None], dw, dgain.reshape(-1)


def solution(mesh):
    tokens = P("blk", "seq", None)
    rows = P(("blk", "seq"), None)
    return jax.shard_map(
        shards,
        mesh=mesh,
        in_specs=(tokens, tokens, tokens, P("blk", "seq"), rows, P()),
        out_specs=(tokens, tokens, tokens, rows, P()),
        check_vma=False,
    )
```

time: 260 us -> 208 us (0.80)
  the two profiles are of different devices: /device:TPU:0 before, /device:TPU:25 now
where the time goes in v2:
time: 208 us
  Pallas kernels  200 us (96%)
  local copies, waits for them, and re-layouts  7.58 us (4%)
    pallas_call x1, Pallas kernels, run_backward(): pl.pallas_call(functools.partial(backward_kernel, n, m, back), name='back...  102 us
    pallas_call x1, Pallas kernels, run_forward(): pl.pallas_call(functools.partial(forward_kernel, n, m, back), name='forwa...  73.9 us
    pallas_call x1, Pallas kernels, run_attention(): pl.pallas_call(functools.partial(attention_kernel, group), name='attentio...  23.6 us
    unnamed x7, local copies, waits for them, and re-layouts  5.55 us

profile of v2, /device:TPU:25, one launch (start us, length us, event | category | flops | bytes accessed | tf_op | source)
XLA Modules:
  0.0 208.1 jit_solution(8701492675662177981)
XLA Ops:
  0.6 0.0 copy-start.1
  0.6 1.3 broadcast_in_dim.26.doc_ref
  2.0 73.9 %forward_exchange.1 = (bf16[4,128,2048]{2,1,0:T(8,128)(2,1)}, bf16[2048,1024]{1,0:T(8,128)(2,1)}, bf16[3,128,1024]{2,1,0:T(8,128)(2,1)}, s32[3,8,128]{2,1,0:T(8,128)}) custom-call(bf16[128,8192]{1,0:T(8,128)(2,1)} %bitcast.10, f32[1,8192]{1,0:T(1,128)} %bitcast.15, bf16[256,1024]{1,0:T(8,128)(2,1)} %w_ref.1, s32[8,128]{1,0:T(8,128)} %broadcast_in_dim.26.doc_ref), custom_call_target="tpu_custom_call" | custom-call | tf_op jit(solution)/shard_map/forward_exchange/pallas_call | solution.py:284
  75.8 0.0 copy-done.1
  75.9 0.7 broadcast_in_dim.27.doc_ref
  76.6 23.6 %attention.1 = (bf16[128,4096]{1,0:T(8,128)(2,1)}, bf16[128,4096]{1,0:T(8,128)(2,1)}, f32[2,128,512]{2,1,0:T(8,128)}, bf16[2,2,128,512]{3,2,1,0:T(8,128)(2,1)}) custom-call(bf16[128,4096]{1,0:T(8,128)(2,1)} %bitcast.13, bf16[128,4096]{1,0:T(8,128)(2,1)} %bitcast.14, bf16[3,128,1024]{2,1,0:T(8,128)(2,1)} %get-tuple-element.16.k_ref.v_ref, ...), custom_call_target="tpu_custom_call" | custom-call | tf_op jit(solution)/shard_map/attention/pallas_call | solution.py:373
  100.2 102.4 %backward_exchange.1 = (bf16[128,8192]{1,0:T(8,128)(2,1)}, f32[256,1024]{1,0:T(8,128)}, f32[32,256]{1,0:T(8,128)}) custom-call(bf16[128,8192]{1,0:T(8,128)(2,1)} %bitcast.11, f32[1,8192]{1,0:T(1,128)} %bitcast.16, bf16[4,128,2048]{2,1,0:T(8,128)(2,1)} %get-tuple-element.20.cols_in, bf16[2048,1024]{1,0:T(8,128)(2,1)} %get-tuple-element.21.slab_in, ...), custom_call_target="tpu_custom_call" | custom-call | tf_op jit(solution)/shard_map/backward_exchange/pallas_call | solution.py:612
  202.5 1.4 copy.11
  203.9 0.0 copy-start
  203.9 3.2 %copy.14 = bf16[1,128,8192]{2,1,0:T(8,128)(2,1)} copy(bf16[1,128,8192]{2,1,0:T(8,128)(2,1)} %bitcast.12) | data formatting | bytes 4194304
  207.1 0.0 copy-done
  207.1 1.0 copy.15
Async XLA Ops:
  0.6 75.2 %copy-start.1 = (s32[1,128]{1,0:T(1,128)S(1)}, s32[1,128]{1,0:T(1,128)}, u32[]{:S(2)}) copy-start(s32[1,128]{1,0:T(1,128)} %param.9) | copy-start | bytes 1540
  203.9 3.2 %copy-start = (f32[256,1024]{1,0:T(8,128)S(1)}, f32[256,1024]{1,0:T(8,128)}, u32[]{:S(2)}) copy-start(f32[256,1024]{1,0:T(8,128)} %get-tuple-element.35) | copy-start | bytes 3145732

commit v3 on v2

--- a/solution.py
+++ b/solution.py
@@ -84,28 +84,89 @@
     def rows(of_core, of_seq):
         return pl.ds(pl.multiple_of((of_core * n + of_seq) * piece, piece), piece)
 
+    kvw = slab.shape[2]
     up, down = lax.rem(s + 1, n), lax.rem(s + n - 1, n)
-    own_rows = rows(core, s)
-    first = remote(w_ref, slab.at[own_rows], fsend.at[0], frecv.at[0], blk=partner)
-
-    def hop(source, sender, sems, i, target):
-        at = rows(core, source)
-        return remote(slab.at[at] if i else w_ref, slab.at[at], sems[0].at[i], sems[1].at[i], seq=target)
-
-    going_up = [hop(lax.rem(s - i + n, n), s, (usend, urecv), i, up) for i in range(n - 1)]
-    going_down = [hop(lax.rem(s + i, n), s, (dsend, drecv), i, down) for i in range(n - 1)]
-
-    @pl.when(s + 1 < n)
-    def _():
-        going_up[0].start()
-
-    @pl.when(s >= 1)
-    def _():
-        going_down[0].start()
-
-    first.start()
-    mine = pltpu.make_async_copy(w_ref, slab.at[own_rows], lsem.at[0])
-    mine.start()
+
+    def part(ref, h):
+        return ref.at[:, pl.ds(h * kvw, kvw)]
+
+    firsts, mines, going_up, going_down, to_partner = [], [], [], [], []
+    for h in range(2):
+        own_rows = rows(core, s)
+        firsts.append(
+            remote(
+                part(w_ref, h), slab.at[h, own_rows], fsend.at[h, 0], frecv.at[h, 0], blk=partner
+            )
+        )
+        mines.append(
+            pltpu.make_async_copy(part(w_ref, h), slab.at[h, own_rows], lsem.at[2 + h])
+        )
+
+        def hop(source, sems, i, target, h=h):
+            at = slab.at[h, rows(core, source)]
+            return remote(
+                at if i else part(w_ref, h), at, sems[0].at[h, i], sems[1].at[h, i], seq=target
+            )
+
+        going_up.append(
+            [hop(lax.rem(s - i + n, n), (usend, urecv), i, up) for i in range(n - 1)]
+        )
+        going_down.append(
+            [hop(lax.rem(s + i, n), (dsend, drecv), i, down) for i in range(n - 1)]
+        )
+
+    def set_out(h):
+        @pl.when(s + 1 < n)
+        def _():
+            going_up[h][0].start()
+
+        @pl.when(s >= 1)
+        def _():
+            going_down[h][0].start()
+
+        firsts[h].start()
+        mines[h].start()
+
+    def pass_on(h):
+        there = []
+        for i in range(1, n):
+            for side, sems, chain, at_edge, more in (
+                (-1, (usend, urecv), going_up[h], s - i >= 0, s + 1 < n),
+                (1, (dsend, drecv), going_down[h], s + i < n, s >= 1),
+            ):
+                source = lax.rem(s + side * i + n, n)
+                slot = i if side < 0 else n - 1 + i
+                shard = slab.at[h, rows(core, source)]
+                copy = remote(shard, shard, fsend.at[h, slot], frecv.at[h, slot], blk=partner)
+                there.append((copy, at_edge))
+
+                @pl.when(at_edge)
+                def _(copy=copy, sems=sems, chain=chain, shard=shard, i=i, more=more, side=side):
+                    remote(
+                        shard, shard, sems[0].at[h, i - 1], sems[1].at[h, i - 1],
+                        seq=up if side < 0 else down,
+                    ).wait_recv()
+                    if i < n - 1:
+
+                        @pl.when(more)
+                        def _():
+                            chain[i].start()
+
+                    copy.start()
+
+        to_partner.extend(there)
+        return there
+
+    def settle(h, there):
+        mines[h].wait()
+        firsts[h].wait_recv()
+        for copy, at_edge in there:
+
+            @pl.when(at_edge)
+            def _(copy=copy):
+                copy.wait_recv()
+
+    set_out(0)
 
     doc_copies = []
     for j in range(1, back + 1):
@@ -147,99 +208,87 @@
             docs_ref[j] = jnp.full(docs_ref.shape[1:], -1, jnp.int32)
             kv_ref[j] = jnp.zeros(kv_ref.shape[1:], BF16)
 
-    mine.wait()
-    to_partner = []
-    for i in range(1, n):
-        for side, sems, chain, at_edge in (
-            (-1, (usend, urecv), going_up, s - i >= 0),
-            (1, (dsend, drecv), going_down, s + i < n),
-        ):
-            source = lax.rem(s + side * i + n, n)
-            slot = i if side < 0 else n - 1 + i
-            shard = slab.at[rows(core, source)]
-            copy = remote(shard, shard, fsend.at[slot], frecv.at[slot], blk=partner)
-            to_partner.append((copy, at_edge))
-            more = (s + 1 < n) if side < 0 else (s >= 1)
-
-            @pl.when(at_edge)
-            def _(copy=copy, sems=sems, chain=chain, shard=shard, i=i, more=more, side=side):
-                remote(
-                    shard, shard, sems[0].at[i - 1], sems[1].at[i - 1], seq=up if side < 0 else down
-                ).wait_recv()
-                if i < n - 1:
-
-                    @pl.when(more)
-                    def _():
-                        chain[i].start()
-
-                copy.start()
-
-    first.wait_recv()
-    for copy, there in to_partner:
-
-        @pl.when(there)
-        def _(copy=copy):
-            copy.wait_recv()
-
-    keep = [pltpu.make_async_copy(slab, slab_out, lsem.at[0])]
-    keep[0].start()
-
-    def project(source, target):
+    def project(h, source, target):
         def one(t, carry):
             at = lanes(t, 256)
-            target[:, at] = jnp.dot(cols[source], slab[:, at], preferred_element_type=F32)
+            target[:, at] = jnp.dot(cols[source], slab[h, :, at], preferred_element_type=F32)
             return carry
 
-        lax.fori_loop(0, target.shape[1] // 256, one, 0)
+        lax.fori_loop(0, kvw // 256, one, 0)
+
+    def arrived(k):
+        source = lax.rem(chip - k + half, half)
+        return remote(
+            send.at[k - 1], cols.at[source], asend.at[k], arecv.at[k], blk=lax.rem(b - 2 * k + m, m)
+        )
 
     sums = []
-    for k in range(1, half):
-        source = lax.rem(chip - k + half, half)
-        back_to = lax.rem(b - 2 * k + m, m)
-        remote(send.at[k - 1], cols.at[source], asend.at[k], arecv.at[k], blk=back_to).wait_recv()
-        project(source, psend.at[k - 1])
-        copy = remote(psend.at[k - 1], precv.at[k - 1], rsend.at[k], rrecv.at[k], blk=back_to)
-        copy.start()
-        sums.append(copy)
-    keep.append(pltpu.make_async_copy(cols, cols_out, lsem.at[1]))
+
+    def project_half(h):
+        sums.append([])
+        for k in range(1, half):
+            if h == 0:
+                arrived(k).wait_recv()
+            project(h, lax.rem(chip - k + half, half), psend.at[h, k - 1])
+            copy = remote(
+                psend.at[h, k - 1], precv.at[h, k - 1], rsend.at[h, k], rrecv.at[h, k],
+                blk=lax.rem(b - 2 * k + m, m),
+            )
+            copy.start()
+            sums[h].append(copy)
+        project(h, chip, own.at[h])
+
+    kv_copies = [
+        [
+            remote(kv_ref.at[j, h], kv_ref.at[j + 1, h], ksend.at[h, j], krecv.at[h, j], seq=up)
+            for j in range(back)
+        ]
+        for h in range(2)
+    ]
+
+    def add_half(h):
+        for copy in sums[h]:
+            copy.wait_recv()
+        total = own[h]
+        for k in range(1, half):
+            total = total + precv[h, k - 1]
+        kv_ref[0, h] = total.astype(BF16)
+
+        @pl.when(s + 1 < n)
+        def _():
+            kv_copies[h][0].start()
+
+    there = pass_on(0)
+    set_out(1)
+    settle(0, there)
+    project_half(0)
+    keep = [pltpu.make_async_copy(cols, cols_out, lsem.at[1])]
+    keep[0].start()
+    there = pass_on(1)
+    settle(1, there)
+    keep.append(pltpu.make_async_copy(slab, slab_out, lsem.at[0]))
     keep[1].start()
-    project(chip, own)
-    for copy in sums:
-        copy.wait_recv()
-
-    def add_up(t, carry):
-        at = lanes(t, 256)
-        total = own[:, at]
-        for k in range(1, half):
-            total = total + precv[k - 1, :, at]
-        kv_ref[0, :, at] = total.astype(BF16)
-        return carry
-
-    lax.fori_loop(0, own.shape[1] // 256, add_up, 0)
-    kv_copies = [
-        remote(kv_ref.at[j], kv_ref.at[j + 1], ksend.at[j], krecv.at[j], seq=up)
-        for j in range(back)
-    ]
+    project_half(1)
+    add_half(0)
+    add_half(1)
+    for j in range(1, back + 1):
+        for h in range(2):
+
+            @pl.when(s - j >= 0)
+            def _(j=j, h=h):
+                kv_copies[h][j - 1].wait_recv()
+                if j < back:
+
+                    @pl.when(s + 1 < n)
+                    def _():
+                        kv_copies[h][j].start()
+
     for j in range(back):
-        if j:
-
-            @pl.when(s - j >= 0)
-            def _(j=j):
-                kv_copies[j - 1].wait_recv()
 
         @pl.when((s - j >= 0) & (s + 1 < n))
         def _(j=j):
-            kv_copies[j].start()
-
-    @pl.when(s - back >= 0)
-    def _():
-        kv_copies[back - 1].wait_recv()
-
-    for j in range(back):
-
-        @pl.when((s - j >= 0) & (s + 1 < n))
-        def _(j=j):
-            kv_copies[j].wait_send()
+            kv_copies[0][j].wait_send()
+            kv_copies[1][j].wait_send()
 
     for j in range(1, back + 1):
 
@@ -255,11 +304,13 @@
 
         @pl.when((s - i >= 0) & (s + 1 < n))
         def _(i=i):
-            going_up[i].wait_send()
+            going_up[0][i].wait_send()
+            going_up[1][i].wait_send()
 
         @pl.when((s + i < n) & (s >= 1))
         def _(i=i):
-            going_down[i].wait_send()
+            going_down[0][i].wait_send()
+            going_down[1][i].wait_send()
 
     for copy, there in to_partner:
 
@@ -267,7 +318,7 @@
         def _(copy=copy):
             copy.wait_send()
 
-    for copy in [first] + out_copies + sums:
+    for copy in firsts + out_copies + sums[0] + sums[1]:
         copy.wait_send()
     for copy in keep:
         copy.wait()
@@ -286,8 +337,8 @@
         name="forward_exchange",
         out_shape=(
             jax.ShapeDtypeStruct((half, tok, wide), BF16),
-            jax.ShapeDtypeStruct((wide, kvc), BF16),
-            jax.ShapeDtypeStruct((back + 1, tok, kvc), BF16),
+            jax.ShapeDtypeStruct((2, wide, kvc // 2), BF16),
+            jax.ShapeDtypeStruct((back + 1, 2, tok, kvc // 2), BF16),
             jax.ShapeDtypeStruct((back + 1,) + docs.shape, jnp.int32),
         ),
         in_specs=[vmem] * 4,
@@ -295,15 +346,15 @@
         scratch_shapes=[
             pltpu.VMEM((half, tok, wide), BF16),
             pltpu.VMEM((half - 1, tok, wide), BF16),
-            pltpu.VMEM((wide, kvc), BF16),
-            pltpu.VMEM((tok, kvc), F32),
-            pltpu.VMEM((half - 1, tok, kvc), F32),
-            pltpu.VMEM((half - 1, tok, kvc), F32),
-            dma((n,)), dma((n,)), dma((n,)), dma((n,)),
-            dma((2 * n,)), dma((2 * n,)),
-            dma((half,)), dma((half,)), dma((half,)), dma((half,)),
-            dma((n,)), dma((n,)), dma((n,)), dma((n,)),
-            dma((2,)),
+            pltpu.VMEM((2, wide, kvc // 2), BF16),
+            pltpu.VMEM((2, tok, kvc // 2), F32),
+            pltpu.VMEM((2, half - 1, tok, kvc // 2), F32),
+            pltpu.VMEM((2, half - 1, tok, kvc // 2), F32),
+            dma((2, n)), dma((2, n)), dma((2, n)), dma((2, n)),
+            dma((2, 2 * n)), dma((2, 2 * n)),
+            dma((half,)), dma((half,)), dma((2, half)), dma((2, half)),
+            dma((2, n)), dma((2, n)), dma((n,)), dma((n,)),
+            dma((4,)),
         ],
         compiler_params=pltpu.CompilerParams(
             collective_id=0, has_side_effects=True, vmem_limit_bytes=VMEM_LIMIT
@@ -314,7 +365,7 @@
 def attention_kernel(
     group, q_ref, g_ref, k_ref, v_ref, docs_ref, doc_ref, att_ref, dq_ref, own_ref, far_ref, dk, dv
 ):
-    slots, tok = k_ref.shape[0], k_ref.shape[1]
+    slots, tok = k_ref.shape[0], k_ref.shape[2]
     keys = slots * tok
     scale = HEAD ** (-0.5)
     k = k_ref[...].reshape(keys, HEAD)
@@ -365,8 +416,8 @@
 
 
 def run_attention(q, g, kv, docs, doc_col):
-    slots, tok, kvc = kv.shape
-    heads = kvc // 2 // HEAD
+    slots, _, tok, kvw = kv.shape
+    heads = kvw // HEAD
     group = q.shape[1] // HEAD // heads
     gw = group * HEAD
     wide = pl.BlockSpec((tok, gw), lambda i: (0, i))
@@ -377,14 +428,14 @@
         out_shape=(
             jax.ShapeDtypeStruct(q.shape, BF16),
             jax.ShapeDtypeStruct(q.shape, BF16),
-            jax.ShapeDtypeStruct((2, tok, kvc // 2), F32),
-            jax.ShapeDtypeStruct((slots - 1, 2, tok, kvc // 2), BF16),
+            jax.ShapeDtypeStruct((2, tok, kvw), F32),
+            jax.ShapeDtypeStruct((slots - 1, 2, tok, kvw), BF16),
         ),
         in_specs=[
             wide,
             wide,
-            pl.BlockSpec((slots, tok, HEAD), lambda i: (0, 0, i)),
-            pl.BlockSpec((slots, tok, HEAD), lambda i: (0, 0, i + heads)),
+            pl.BlockSpec((slots, 1, tok, HEAD), lambda i: (0, 0, 0, i)),
+            pl.BlockSpec((slots, 1, tok, HEAD), lambda i: (0, 1, 0, i)),
             pl.BlockSpec(docs.shape, lambda i: (0, 0, 0)),
             pl.BlockSpec(doc_col.shape, lambda i: (0, 0)),
         ],
@@ -426,95 +477,117 @@
         copy.start()
     greet(n, m)
     far_copies = []
-    for j in range(1, back + 1):
-        copy = remote(
-            far_ref.at[j - 1], far_buf.at[j - 1], psend.at[j], precv.at[j],
-            seq=lax.rem(s - j + n, n),
-        )
-        far_copies.append(copy)
-
-        @pl.when(s - j >= 0)
-        def _(copy=copy):
+    for h in range(2):
+        far_copies.append([])
+        for j in range(1, back + 1):
+            copy = remote(
+                far_ref.at[j - 1, h], far_buf.at[j - 1, h], psend.at[h, j], precv.at[h, j],
+                seq=lax.rem(s - j + n, n),
+            )
+            far_copies[h].append(copy)
+
+            @pl.when(s - j >= 0)
+            def _(copy=copy):
+                copy.start()
+
+            @pl.when(s + j >= n)
+            def _(j=j, h=h):
+                far_buf[j - 1, h] = jnp.zeros(far_buf.shape[2:], BF16)
+
+    inv = inverse_rms(x_ref)
+    gather = []
+
+    def sum_half(h):
+        for j in range(1, back + 1):
+
+            @pl.when(s + j < n)
+            def _(j=j):
+                far_copies[h][j - 1].wait_recv()
+
+        total = own_ref[h]
+        for j in range(1, back + 1):
+            total = total + far_buf[j - 1, h].astype(F32)
+        gkv[h, chip] = total.astype(BF16)
+        for k in range(1, half):
+            copy = remote(
+                gkv.at[h, chip], gkv.at[h, chip], gsend.at[h, k], grecv.at[h, k],
+                blk=lax.rem(b + 2 * k, m),
+            )
             copy.start()
-
-        @pl.when(s + j >= n)
-        def _(j=j):
-            far_buf[j - 1] = jnp.zeros(far_buf.shape[1:], BF16)
-
-    inv = inverse_rms(x_ref)
-    for j in range(1, back + 1):
-
-        @pl.when(s + j < n)
-        def _(j=j):
-            far_copies[j - 1].wait_recv()
-
-    for part in range(2):
-        total = own_ref[part]
-        for j in range(1, back + 1):
-            total = total + far_buf[j - 1, part].astype(F32)
-        gkv[chip, :, part * kvw : (part + 1) * kvw] = total.astype(BF16)
-    gather = []
-    for k in range(1, half):
-        copy = remote(
-            gkv.at[chip], gkv.at[chip], gsend.at[k], grecv.at[k], blk=lax.rem(b + 2 * k, m)
-        )
-        copy.start()
-        gather.append(copy)
-    for copy in loads:
-        copy.wait()
+            gather.append(copy)
+
+    tile = 256
+    tiles = n * piece // tile
+
+    def weight_tile(h, of_core, t):
+        left = cols[:, :, lanes(of_core * tiles + t, tile)].reshape(half * tok, tile)
+        return lax.dot_general(
+            left, gkv[h].reshape(half * tok, kvw), (((0,), (0,)), ((), ())),
+            preferred_element_type=F32,
+        )
+
+    pair_copies = [[], []]
+
+    def weight_half(h):
+        for k in range(1, half):
+            source = lax.rem(chip - k + half, half)
+            remote(
+                gkv.at[h, chip], gkv.at[h, source], gsend.at[h, k], grecv.at[h, k],
+                blk=lax.rem(b - 2 * k + m, m),
+            ).wait_recv()
+        for t in range(tiles):
+            at = pl.ds(t * tile, tile)
+            pair_send[h, at] = weight_tile(h, 1 - core, t).astype(BF16)
+            copy = remote(
+                pair_send.at[h, at], pair_recv.at[h, at], csend.at[h, t], crecv.at[h, t], blk=partner
+            )
+            copy.start()
+            pair_copies[h].append(copy)
+
+        def kept(t, carry):
+            at = pl.ds(pl.multiple_of(t * tile, tile), tile)
+            keep[h, at] = weight_tile(h, core, t)
+            return carry
+
+        lax.fori_loop(0, tiles, kept, 0)
+
+    owner_copies = [[], []]
+
+    def send_half(h):
+        for copy in pair_copies[h]:
+            copy.wait_recv()
+        for j in far_first(n):
+            target = lax.rem(s + j, n)
+            at = pl.ds(pl.multiple_of(target * piece, piece), piece)
+            osend[h, j - 1] = (keep[h, at] + pair_recv[h, at].astype(F32)).astype(BF16)
+            copy = remote(
+                osend.at[h, j - 1], orecv.at[h, j - 1], wsend.at[h, j], wrecv.at[h, j], seq=target
+            )
+            copy.start()
+            owner_copies[h].append(copy)
 
     def to_normed(source, ref):
         def one(t, carry):
             rows = pl.ds(pl.multiple_of(t * 256, 256), 256)
-            ref[:, lanes(t, 256)] = lax.dot_general(
-                gkv[source], slab[rows, :], (((1,), (1,)), ((), ())),
-                preferred_element_type=F32,
-            ).astype(BF16)
+            terms = [
+                lax.dot_general(
+                    gkv[h, source], slab[h, rows, :], (((1,), (1,)), ((), ())),
+                    preferred_element_type=F32,
+                )
+                for h in range(2)
+            ]
+            ref[:, lanes(t, 256)] = (terms[0] + terms[1]).astype(BF16)
             return carry
 
         lax.fori_loop(0, wide // 256, one, 0)
 
-    to_normed(chip, nrecv.at[chip])
-    for k in range(1, half):
-        source = lax.rem(chip - k + half, half)
-        remote(
-            gkv.at[chip], gkv.at[source], gsend.at[k], grecv.at[k], blk=lax.rem(b - 2 * k + m, m)
-        ).wait_recv()
-
-    tile = 256
-    tiles = n * piece // tile
-
-    def weight_tile(of_core, t):
-        left = cols[:, :, lanes(of_core * tiles + t, tile)].reshape(half * tok, tile)
-        return lax.dot_general(
-            left, gkv[...].reshape(half * tok, 2 * kvw), (((0,), (0,)), ((), ())),
-            preferred_element_type=F32,
-        )
-
-    pair_copies = []
-    for t in range(tiles):
-        at = pl.ds(t * tile, tile)
-        pair_send[at] = weight_tile(1 - core, t).astype(BF16)
-        copy = remote(pair_send.at[at], pair_recv.at[at], csend.at[t], crecv.at[t], blk=partner)
-        copy.start()
-        pair_copies.append(copy)
-
-    def kept(t, carry):
-        keep[pl.ds(pl.multiple_of(t * tile, tile), tile)] = weight_tile(core, t)
-        return carry
-
-    lax.fori_loop(0, tiles, kept, 0)
-    for copy in pair_copies:
-        copy.wait_recv()
-    owner_copies = []
-    for j in far_first(n):
-        target = lax.rem(s + j, n)
-        at = pl.ds(pl.multiple_of(target * piece, piece), piece)
-        osend[j - 1] = (keep[at] + pair_recv[at].astype(F32)).astype(BF16)
-        copy = remote(osend.at[j - 1], orecv.at[j - 1], wsend.at[j], wrecv.at[j], seq=target)
-        copy.start()
-        owner_copies.append(copy)
-
+    sum_half(0)
+    for copy in loads:
+        copy.wait()
+    weight_half(0)
+    sum_half(1)
+    send_half(0)
+    weight_half(1)
     normed_copies = []
     for k in range(1, half):
         source = lax.rem(chip - k + half, half)
@@ -524,6 +597,8 @@
         )
         copy.start()
         normed_copies.append(copy)
+    send_half(1)
+    to_normed(chip, nrecv.at[chip])
 
     for k in range(1, half):
         source = lax.rem(chip + k, half)
@@ -575,14 +650,14 @@
         )
         copy.start()
         blk_copies.append(copy)
-    for copy in owner_copies:
-        copy.wait_recv()
-
     at = pl.ds(pl.multiple_of(s * piece, piece), piece)
-    dw = keep[at] + pair_recv[at].astype(F32)
-    for j in range(1, n):
-        dw = dw + orecv[j - 1].astype(F32)
-    dw_ref[...] = dw
+    for h in range(2):
+        for copy in owner_copies[h]:
+            copy.wait_recv()
+        dw = keep[h, at] + pair_recv[h, at].astype(F32)
+        for j in range(1, n):
+            dw = dw + orecv[h, j - 1].astype(F32)
+        dw_ref[:, h * kvw : (h + 1) * kvw] = dw
     for j in range(1, m):
         source = lax.rem(b - j + m, m)
         remote(
@@ -592,18 +667,23 @@
     for i in range(1, m):
         gain_sum = gain_sum + blk_gain[i]
     dgain_ref[...] = gain_sum
-    for copy in gather + normed_copies + pair_copies + owner_copies + seq_copies + blk_copies:
+    for copy in (
+        gather + normed_copies + pair_copies[0] + pair_copies[1]
+        + owner_copies[0] + owner_copies[1] + seq_copies + blk_copies
+    ):
         copy.wait_send()
     for j in range(1, back + 1):
 
         @pl.when(s - j >= 0)
         def _(j=j):
-            far_copies[j - 1].wait_send()
+            far_copies[0][j - 1].wait_send()
+            far_copies[1][j - 1].wait_send()
 
 
 def run_backward(n, m, back, piece, x, gain, cols, slab, own, far):
     tok, width = x.shape
-    wide, kvc = slab.shape
+    _, wide, kvw = slab.shape
+    kvc = 2 * kvw
     dma = pltpu.SemaphoreType.DMA
     vmem = pl.BlockSpec(memory_space=pltpu.VMEM)
     hbm = pl.BlockSpec(memory_space=pl.ANY)
@@ -623,18 +703,18 @@
             pltpu.VMEM(cols.shape, BF16),
             pltpu.VMEM(slab.shape, BF16),
             pltpu.VMEM(far.shape, BF16),
-            pltpu.VMEM((half, tok, kvc), BF16),
+            pltpu.VMEM((2, half, tok, kvw), BF16),
             pltpu.VMEM((half - 1, tok, wide), BF16),
             pltpu.VMEM((half, tok, wide), BF16),
-            pltpu.VMEM((n * piece, kvc), BF16),
-            pltpu.VMEM((n * piece, kvc), BF16),
-            pltpu.VMEM((n * piece, kvc), F32),
-            pltpu.VMEM((n - 1, piece, kvc), BF16),
-            pltpu.VMEM((n - 1, piece, kvc), BF16),
+            pltpu.VMEM((2, n * piece, kvw), BF16),
+            pltpu.VMEM((2, n * piece, kvw), BF16),
+            pltpu.VMEM((2, n * piece, kvw), F32),
+            pltpu.VMEM((2, n - 1, piece, kvw), BF16),
+            pltpu.VMEM((2, n - 1, piece, kvw), BF16),
             pltpu.VMEM((n,) + gains, F32),
             pltpu.VMEM((m,) + gains, F32),
-            dma((n,)), dma((n,)), dma((half,)), dma((half,)), dma((half,)), dma((half,)),
-            dma((n,)), dma((n,)), dma((n,)), dma((n,)),
+            dma((2, n)), dma((2, n)), dma((2, half)), dma((2, half)), dma((half,)), dma((half,)),
+            dma((2, n)), dma((2, n)), dma((2, n)), dma((2, n)),
             dma((n,)), dma((n,)), dma((m,)), dma((m,)),
             dma((2,)),
         ],

time: 208 us -> 192 us (0.923)
  the two profiles are of different devices: /device:TPU:25 before, /device:TPU:0 now
where the time goes in v3:
time: 192 us; the launch traced here: 191 us
  Pallas kernels  183 us (95%)
  local copies, waits for them, and re-layouts  7.58 us (4%)
    pallas_call x1, Pallas kernels, run_backward(): pl.pallas_call(functools.partial(backward_kernel, n, m, back), name='back...  90.8 us
    pallas_call x1, Pallas kernels, run_forward(): pl.pallas_call(functools.partial(forward_kernel, n, m, back), name='forwa...  68.3 us
    pallas_call x1, Pallas kernels, run_attention(): pl.pallas_call(functools.partial(attention_kernel, group), name='attentio...  23.5 us
    unnamed x7, local copies, waits for them, and re-layouts  5.55 us

profile of v3, /device:TPU:0, one launch (start us, length us, event | category | flops | bytes accessed | tf_op | source)
XLA Modules:
  0.0 190.8 jit_solution(15597761150520458489)
XLA Ops:
  0.6 0.0 copy-start.1
  0.6 1.3 broadcast_in_dim.26.doc_ref
  2.0 68.3 %forward_exchange.1 = (bf16[4,128,2048]{2,1,0:T(8,128)(2,1)}, bf16[2,2048,512]{2,1,0:T(8,128)(2,1)}, bf16[3,2,128,512]{3,2,1,0:T(8,128)(2,1)}, s32[3,8,128]{2,1,0:T(8,128)}) custom-call(bf16[128,8192]{1,0:T(8,128)(2,1)} %bitcast.10, f32[1,8192]{1,0:T(1,128)} %bitcast.15, bf16[256,1024]{1,0:T(8,128)(2,1)} %w_ref.1, s32[8,128]{1,0:T(8,128)} %broadcast_in_dim.26.doc_ref), custom_call_target="tpu_custom_call" | custom-call | tf_op jit(solution)/shard_map/forward_exchange/pallas_call | solution.py:335
  70.2 0.0 copy-done.1
  70.2 0.7 broadcast_in_dim.27.doc_ref
  70.9 23.5 %attention.1 = (bf16[128,4096]{1,0:T(8,128)(2,1)}, bf16[128,4096]{1,0:T(8,128)(2,1)}, f32[2,128,512]{2,1,0:T(8,128)}, bf16[2,2,128,512]{3,2,1,0:T(8,128)(2,1)}) custom-call(bf16[128,4096]{1,0:T(8,128)(2,1)} %bitcast.13, bf16[128,4096]{1,0:T(8,128)(2,1)} %bitcast.14, bf16[3,2,128,512]{3,2,1,0:T(8,128)(2,1)} %get-tuple-element.16.k_ref.v_ref, ...), custom_call_target="tpu_custom_call" | custom-call | tf_op jit(solution)/shard_map/attention/pallas_call | solution.py:424
  94.5 90.8 %backward_exchange.1 = (bf16[128,8192]{1,0:T(8,128)(2,1)}, f32[256,1024]{1,0:T(8,128)}, f32[32,256]{1,0:T(8,128)}) custom-call(bf16[128,8192]{1,0:T(8,128)(2,1)} %bitcast.11, f32[1,8192]{1,0:T(1,128)} %bitcast.16, bf16[4,128,2048]{2,1,0:T(8,128)(2,1)} %get-tuple-element.20.cols_in, bf16[2,2048,512]{2,1,0:T(8,128)(2,1)} %get-tuple-element.21.slab_in, ...), custom_call_target="tpu_custom_call" | custom-call | tf_op jit(solution)/shard_map/backward_exchange/pallas_call | solution.py:692
  185.3 1.4 copy.11
  186.6 0.0 copy-start
  186.6 3.2 %copy.14 = bf16[1,128,8192]{2,1,0:T(8,128)(2,1)} copy(bf16[1,128,8192]{2,1,0:T(8,128)(2,1)} %bitcast.12) | data formatting | bytes 4194304
  189.8 0.0 copy-done
  189.8 1.0 copy.15
Async XLA Ops:
  0.6 69.6 %copy-start.1 = (s32[1,128]{1,0:T(1,128)S(1)}, s32[1,128]{1,0:T(1,128)}, u32[]{:S(2)}) copy-start(s32[1,128]{1,0:T(1,128)} %param.9) | copy-start | bytes 1540
  186.6 3.2 %copy-start = (f32[256,1024]{1,0:T(8,128)S(1)}, f32[256,1024]{1,0:T(8,128)}, u32[]{:S(2)}) copy-start(f32[256,1024]{1,0:T(8,128)} %get-tuple-element.35) | copy-start | bytes 3145732

commit v4 on v3

--- a/solution.py
+++ b/solution.py
@@ -363,7 +363,8 @@
 
 
 def attention_kernel(
-    group, q_ref, g_ref, k_ref, v_ref, docs_ref, doc_ref, att_ref, dq_ref, own_ref, far_ref, dk, dv
+    group, q_ref, g_ref, k_ref, v_ref, docs_ref, doc_ref, att_ref, dq_ref, own_ref, far_ref, dk, dv,
+    pst, dst, qst, gst,
 ):
     slots, tok = k_ref.shape[0], k_ref.shape[2]
     keys = slots * tok
@@ -378,8 +379,6 @@
         parts.append(docs_ref[j, 0:1, :] == mine)
     bias = jnp.concatenate([jnp.where(p, 1.0, 0.0).astype(F32) for p in parts], axis=1)
     allowed = bias > 0.5
-    dk[...] = jnp.zeros_like(dk)
-    dv[...] = jnp.zeros_like(dv)
     nt = (((1,), (1,)), ((), ()))
     tn = (((0,), (0,)), ((), ()))
 
@@ -400,14 +399,19 @@
         probs = expo * inv
         gp = lax.dot_general(g, v, nt, preferred_element_type=F32)
         ds = (probs * (gp - delta)).astype(BF16)
-        dv[...] += lax.dot_general(probs.astype(BF16), g, tn, preferred_element_type=F32)
-        dk[...] += lax.dot_general(ds, q, tn, preferred_element_type=F32)
+        rows = pl.ds(pl.multiple_of(h * tok, tok), tok)
+        pst[rows, :] = probs.astype(BF16)
+        dst[rows, :] = ds
+        qst[rows, :] = q
+        gst[rows, :] = g
         dq_ref[:, at] = (
             jnp.dot(ds, k, preferred_element_type=F32) * scale
         ).astype(BF16)
         return carry
 
-    lax.fori_loop(0, group, head, 0, unroll=2)
+    lax.fori_loop(0, group, head, 0, unroll=8)
+    dv[...] = lax.dot_general(pst[...], gst[...], tn, preferred_element_type=F32)
+    dk[...] = lax.dot_general(dst[...], qst[...], tn, preferred_element_type=F32)
     own_ref[0] = dk[0:tok, :] * scale
     own_ref[1] = dv[0:tok, :]
     for j in range(1, slots):
@@ -448,6 +452,10 @@
         scratch_shapes=[
             pltpu.VMEM((slots * tok, HEAD), F32),
             pltpu.VMEM((slots * tok, HEAD), F32),
+            pltpu.VMEM((group * tok, slots * tok), BF16),
+            pltpu.VMEM((group * tok, slots * tok), BF16),
+            pltpu.VMEM((group * tok, HEAD), BF16),
+            pltpu.VMEM((group * tok, HEAD), BF16),
         ],
     )(q, g, kv, kv, docs, doc_col)
 
@@ -612,18 +620,18 @@
         at = lanes(i, 256)
         scaled = x_ref[:, at].astype(F32) * inv
         term = nrecv[i // per, :, lanes(lax.rem(i, per), 256)].astype(F32) * scaled
-        seq_gain[s, pl.ds(i, 1), :] = jnp.sum(term, axis=0, keepdims=True)
+        blk_gain[b, pl.ds(i, 1), :] = jnp.sum(term, axis=0, keepdims=True)
         term = term * gain_ref[:, at]
         return total + term[:, :128] + term[:, 128:]
 
-    total = lax.fori_loop(0, width // 256, means, jnp.zeros((tok, 128), F32))
-    seq_copies = []
-    for j in range(1, n):
+    total = lax.fori_loop(0, width // 256, means, jnp.zeros((tok, 128), F32), unroll=2)
+    blk_copies = []
+    for j in range(1, m):
         copy = remote(
-            seq_gain.at[s], seq_gain.at[s], ssend.at[j], srecv.at[j], seq=lax.rem(s + j, n)
+            blk_gain.at[b], blk_gain.at[b], bsend.at[j], brecv.at[j], blk=lax.rem(b + j, m)
         )
         copy.start()
-        seq_copies.append(copy)
+        blk_copies.append(copy)
     mean = jnp.sum(total, axis=1, keepdims=True) / width
 
     def finish(i, carry):
@@ -633,7 +641,32 @@
         dx_ref[:, at] = (inv * (hat - scaled * mean)).astype(BF16)
         return carry
 
-    lax.fori_loop(0, width // 256, finish, 0)
+    lax.fori_loop(0, width // 256, finish, 0, unroll=2)
+    for j in range(1, m):
+        source = lax.rem(b - j + m, m)
+        remote(
+            blk_gain.at[b], blk_gain.at[source], bsend.at[j], brecv.at[j], blk=source
+        ).wait_recv()
+    gain_sum = blk_gain[0]
+    for i in range(1, m):
+        gain_sum = gain_sum + blk_gain[i]
+    seq_gain[s] = gain_sum
+    seq_copies = []
+    for j in range(1, n):
+        copy = remote(
+            seq_gain.at[s], seq_gain.at[s], ssend.at[j], srecv.at[j], seq=lax.rem(s + j, n)
+        )
+        copy.start()
+        seq_copies.append(copy)
+
+    at = pl.ds(pl.multiple_of(s * piece, piece), piece)
+    for h in range(2):
+        for copy in owner_copies[h]:
+            copy.wait_recv()
+        dw = keep[h, at] + pair_recv[h, at].astype(F32)
+        for j in range(1, n):
+            dw = dw + orecv[h, j - 1].astype(F32)
+        dw_ref[:, h * kvw : (h + 1) * kvw] = dw
     for j in range(1, n):
         source = lax.rem(s - j + n, n)
         remote(
@@ -642,30 +675,6 @@
     gain_sum = seq_gain[0]
     for i in range(1, n):
         gain_sum = gain_sum + seq_gain[i]
-    blk_gain[b] = gain_sum
-    blk_copies = []
-    for j in range(1, m):
-        copy = remote(
-            blk_gain.at[b], blk_gain.at[b], bsend.at[j], brecv.at[j], blk=lax.rem(b + j, m)
-        )
-        copy.start()
-        blk_copies.append(copy)
-    at = pl.ds(pl.multiple_of(s * piece, piece), piece)
-    for h in range(2):
-        for copy in owner_copies[h]:
-            copy.wait_recv()
-        dw = keep[h, at] + pair_recv[h, at].astype(F32)
-        for j in range(1, n):
-            dw = dw + orecv[h, j - 1].astype(F32)
-        dw_ref[:, h * kvw : (h + 1) * kvw] = dw
-    for j in range(1, m):
-        source = lax.rem(b - j + m, m)
-        remote(
-            blk_gain.at[b], blk_gain.at[source], bsend.at[j], brecv.at[j], blk=source
-        ).wait_recv()
-    gain_sum = blk_gain[0]
-    for i in range(1, m):
-        gain_sum = gain_sum + blk_gain[i]
     dgain_ref[...] = gain_sum
     for copy in (
         gather + normed_copies + pair_copies[0] + pair_copies[1]

time: 192 us -> 188 us (0.979)
  Pallas kernels: 183 us -> 179 us
    pallas_call x1, Pallas kernels: 23.5 us -> 19.4 us  [run_attention(): pl.pallas_call(functools.partial(attention_kernel, group), name='attentio...]
where the time goes in v4:
time: 188 us
  Pallas kernels  179 us (95%)
  local copies, waits for them, and re-layouts  7.58 us (4%)
    pallas_call x1, Pallas kernels, run_backward(): pl.pallas_call(functools.partial(backward_kernel, n, m, back), name='back...  91.7 us
    pallas_call x1, Pallas kernels, run_forward(): pl.pallas_call(functools.partial(forward_kernel, n, m, back), name='forwa...  68.3 us
    pallas_call x1, Pallas kernels, run_attention(): pl.pallas_call(functools.partial(attention_kernel, group), name='attentio...  19.4 us
    unnamed x7, local copies, waits for them, and re-layouts  5.55 us

profile of v4, /device:TPU:0, one launch (start us, length us, event | category | flops | bytes accessed | tf_op | source)
XLA Modules:
  0.0 187.6 jit_solution(9257770780196255409)
XLA Ops:
  0.6 0.0 copy-start.1
  0.6 1.3 broadcast_in_dim.26.doc_ref
  2.0 68.3 %forward_exchange.1 = (bf16[4,128,2048]{2,1,0:T(8,128)(2,1)}, bf16[2,2048,512]{2,1,0:T(8,128)(2,1)}, bf16[3,2,128,512]{3,2,1,0:T(8,128)(2,1)}, s32[3,8,128]{2,1,0:T(8,128)}) custom-call(bf16[128,8192]{1,0:T(8,128)(2,1)} %bitcast.10, f32[1,8192]{1,0:T(1,128)} %bitcast.15, bf16[256,1024]{1,0:T(8,128)(2,1)} %w_ref.1, s32[8,128]{1,0:T(8,128)} %broadcast_in_dim.26.doc_ref), custom_call_target="tpu_custom_call" | custom-call | tf_op jit(solution)/shard_map/forward_exchange/pallas_call | solution.py:335
  70.2 0.0 copy-done.1
  70.2 0.7 broadcast_in_dim.27.doc_ref
  70.9 19.4 %attention.1 = (bf16[128,4096]{1,0:T(8,128)(2,1)}, bf16[128,4096]{1,0:T(8,128)(2,1)}, f32[2,128,512]{2,1,0:T(8,128)}, bf16[2,2,128,512]{3,2,1,0:T(8,128)(2,1)}) custom-call(bf16[128,4096]{1,0:T(8,128)(2,1)} %bitcast.13, bf16[128,4096]{1,0:T(8,128)(2,1)} %bitcast.14, bf16[3,2,128,512]{3,2,1,0:T(8,128)(2,1)} %get-tuple-element.16.k_ref.v_ref, ...), custom_call_target="tpu_custom_call" | custom-call | tf_op jit(solution)/shard_map/attention/pallas_call | solution.py:428
  90.3 91.7 %backward_exchange.1 = (bf16[128,8192]{1,0:T(8,128)(2,1)}, f32[256,1024]{1,0:T(8,128)}, f32[32,256]{1,0:T(8,128)}) custom-call(bf16[128,8192]{1,0:T(8,128)(2,1)} %bitcast.11, f32[1,8192]{1,0:T(1,128)} %bitcast.16, bf16[4,128,2048]{2,1,0:T(8,128)(2,1)} %get-tuple-element.20.cols_in, bf16[2,2048,512]{2,1,0:T(8,128)(2,1)} %get-tuple-element.21.slab_in, ...), custom_call_target="tpu_custom_call" | custom-call | tf_op jit(solution)/shard_map/backward_exchange/pallas_call | solution.py:701
  182.0 1.4 copy.11
  183.4 0.0 copy-start
  183.4 3.2 %copy.14 = bf16[1,128,8192]{2,1,0:T(8,128)(2,1)} copy(bf16[1,128,8192]{2,1,0:T(8,128)(2,1)} %bitcast.12) | data formatting | bytes 4194304
  186.6 0.0 copy-done
  186.6 1.0 copy.15
Async XLA Ops:
  0.6 69.6 %copy-start.1 = (s32[1,128]{1,0:T(1,128)S(1)}, s32[1,128]{1,0:T(1,128)}, u32[]{:S(2)}) copy-start(s32[1,128]{1,0:T(1,128)} %param.9) | copy-start | bytes 1540
  183.4 3.2 %copy-start = (f32[256,1024]{1,0:T(8,128)S(1)}, f32[256,1024]{1,0:T(8,128)}, u32[]{:S(2)}) copy-start(f32[256,1024]{1,0:T(8,128)} %get-tuple-element.35) | copy-start | bytes 3145732
